TPU v7x, 32 devices: a whole 2x2x4 slice. The times are simulated.
32 devices in a mesh: run: 4 (over x, core), space: 8 (over z, y).
Axes of the slice: x: 2, y: 2, z: 4, core: 2. Of those that a mesh axis runs over, the one named last changes fastest.
Arguments:
- adjoint_init: float32 [4, 3, 32, 192, 256], P('run', None, 'space'), may hold values from -6 to 6
- forward_snaps: bfloat16 [8, 3, 32, 192, 256], P('run', None, 'space'), may hold values from -6 to 6
- base_speed: float32 [192], replicated, may hold values from 0.2 to 1.5
- fwd_times: int32 [8], replicated, may hold values from 0 to 15
- adj_times: int32 [4, 4], P('run'), may hold values from 0 to 15
- horizon: int32 [4], P('run'), may hold values from 8 to 24
Outputs:
- final_adjoint: float32 [4, 3, 32, 192, 256], P('run', None, 'space')
- hankel: float32 [4, 4, 8], P('run')
All inputs are finite; a program needn't handle non-finite values.
Results may differ from a plain program's by a relative error of at most 0.0027.
Values may be sent and summed in bfloat16 or wider, within the bound.
No kernel may reach another device: no remote copies, remote signals or barrier semaphores. Data moves between devices by JAX's collectives and lax.ppermute only.
A program may use at most 128 MiB of HBM per device.

v0:
```python
import functools
import math

import jax
import jax.numpy as jnp
from jax import lax
from jax.experimental import pallas as pl
from jax.experimental.pallas import tpu as pltpu
from jax.sharding import PartitionSpec as P

SNAP = 4
time_step = 0.5
viscosity = 0.2


ROWS = 16
PAD = 8
UNROLL = 6


def in_hbm(array):
    return pltpu.with_memory_space_constraint(array, pltpu.HBM)


def in_vmem(array):
    return pltpu.with_memory_space_constraint(array, pltpu.VMEM)


def cost(us):
    return pl.CostEstimate(flops=0, transcendentals=0, bytes_accessed=int(us * 3.0e6))


def stencil(src, i, rows, east, west, lanes):
    row0 = rows
    centre = [src[i, h, pl.ds(row0, ROWS), :] for h in (0, 1)]
    up = [pltpu.roll(c, 127, 1) for c in centre]
    down = [pltpu.roll(c, 1, 1) for c in centre]
    out = []
    for h in (0, 1):
        above = jnp.where(lanes == 127, up[1 - h], up[h])
        below = jnp.where(lanes == 0, down[1 - h], down[h])
        north = src[i, h, pl.ds(row0 + 1, ROWS), :]
        south = src[i, h, pl.ds(row0 - 1, ROWS), :]
        around = (north + south) + (above + below)
        value = east * src[i + 1, h, pl.ds(row0, ROWS), :] + west * src[i - 1, h, pl.ds(row0, ROWS), :]
        value = value + (time_step * viscosity) * around + (1.0 - 6.0 * time_step * viscosity) * centre[h]
        out.append(value)
    return out


def evolve_kernel(*refs, coupled, keep, planes, ny, at):
    refs = list(refs)
    odd = refs.pop(0)
    coefficients = refs.pop(0)
    east_ref, west_ref, shear_ref = coefficients.at[0], coefficients.at[1], coefficients.at[2]
    own, swapped, shifted = refs.pop(0), refs.pop(0), refs.pop(0)
    others = [refs.pop(0) for _ in range(4)] if coupled else [None] * 4
    new, snaps = refs.pop(0), [refs.pop(0), refs.pop(0)]
    work = [refs.pop(0) for _ in range(4)]
    sems = refs.pop(0)
    steps = ny // ROWS
    n = planes
    copies = []
    for i in range(n):
        for h in (0, 1):
            source = own.at[(*at, i, slice(None), pl.ds(h * 128, 128))]
            copies.append(pltpu.make_async_copy(source, work[0].at[n + i, h, pl.ds(PAD, ny), :], sems.at[2 * i + h]))
    for copy in copies:
        copy.start()
    swap_at = jnp.where(odd[0] == 1, 0, 2 * n)
    shift_at = 2 * n - swap_at
    lanes = lax.broadcasted_iota(jnp.int32, (ROWS, 128), 1)
    zeros = jnp.zeros((PAD, 128), jnp.float32)
    for buffer in work:
        for i in range(buffer.shape[0]):
            for h in (0, 1):
                buffer[i, h, pl.ds(0, PAD), :] = zeros
                buffer[i, h, pl.ds(PAD + ny, PAD), :] = zeros

    def fill(t, _):
        row0 = pl.multiple_of(t * ROWS, ROWS)
        for i in range(n):
            for h in (0, 1):
                cols = pl.ds(h * 128, 128)
                rows = pl.ds(PAD + row0, ROWS)
                work[0][swap_at + i, h, rows, :] = swapped[i, pl.ds(row0, ROWS), cols].astype(jnp.float32)
                work[0][shift_at + i, h, rows, :] = shifted[i, pl.ds(row0, ROWS), cols].astype(jnp.float32)
        return 0

    lax.fori_loop(0, steps, fill, 0, unroll=UNROLL)
    for copy in copies:
        copy.wait()

    for k in range(4):
        src = work[k]
        dst = work[k + 1] if k < 3 else None

        def apply(t, _, k=k, src=src, dst=dst):
            row0 = pl.multiple_of(t * ROWS, ROWS)
            east = east_ref[pl.ds(row0, ROWS), :]
            west = west_ref[pl.ds(row0, ROWS), :]
            for i in range(k + 1, 3 * n - 1 - k):
                value = stencil(src, i - k, PAD + row0, east, west, lanes)
                for h in (0, 1):
                    cols = pl.ds(h * 128, 128)
                    rows = pl.ds(PAD + row0, ROWS)
                    got = value[h]
                    if coupled:
                        got = got - shear_ref[pl.ds(row0, ROWS), :] * others[k][i - k, h, rows, :]
                    if k % 2 == 1:
                        got = 0.5 * (work[k - 1][i - k + 1, h, rows, :] + got)
                    if dst is not None:
                        dst[i - k - 1, h, rows, :] = got
                    if k % 2 == 1 and n <= i < 2 * n:
                        snaps[k // 2][i - n, pl.ds(row0, ROWS), cols] = got.astype(jnp.bfloat16)
                    if k == 3:
                        new[i - n, pl.ds(row0, ROWS), cols] = got
            return 0

        lax.fori_loop(0, steps, apply, 0, unroll=UNROLL)


def evolve(odd, coefficients, own, at, swapped, shifted, others=None, keep=False):
    planes, ny, nz = swapped.shape
    coupled = others is not None
    vmem = pl.BlockSpec(memory_space=pltpu.VMEM)
    kept = [jax.ShapeDtypeStruct((3 * planes - 2 * k, 2, ny + 2 * PAD, 128), jnp.float32) for k in range(4)]
    first = len(at) > 0
    new = (pltpu.VMEM if first else jax.ShapeDtypeStruct)((planes, ny, nz), jnp.float32)
    work = [pltpu.VMEM(s.shape, s.dtype) for s in kept]
    scratch = [] if keep else work
    outs = [new] + [pltpu.VMEM((planes, ny, nz), jnp.bfloat16)] * 2 + (work if keep else [])
    before = [coefficients]
    after = [in_vmem(a) for a in (swapped, shifted) + (tuple(others) if coupled else ())]
    own = in_hbm(own) if first else in_vmem(own)
    return pl.pallas_call(
        functools.partial(evolve_kernel, coupled=coupled, keep=keep, planes=planes, ny=ny, at=at),
        out_shape=outs,
        in_specs=[pl.BlockSpec(memory_space=pltpu.SMEM)]
        + [vmem] * len(before)
        + [pl.BlockSpec(memory_space=pltpu.HBM) if first else vmem]
        + [vmem] * len(after),
        out_specs=[vmem] * len(outs),
        scratch_shapes=scratch + [pltpu.SemaphoreType.DMA((2 * planes,))],
        compiler_params=pltpu.CompilerParams(vmem_limit_bytes=12 * 1024 * 1024),
        cost_estimate=cost(4.5),
        name="evolve_v" if coupled else ("evolve_u" if keep else "evolve_w"),
    )(odd, *before, own, *after)


def round_kernel(fields, after, out, buffer, sems, *, c):
    copies = [pltpu.make_async_copy(fields.at[0, c, i], buffer.at[i], sems.at[i]) for i in range(out.shape[0])]
    for copy in copies:
        copy.start()
    for i, copy in enumerate(copies):
        copy.wait()
        out[i] = buffer[i].astype(jnp.bfloat16)


def rounded(fields, c, after):
    _, _, planes, ny, nz = fields.shape
    return pl.pallas_call(
        functools.partial(round_kernel, c=c),
        out_shape=pltpu.VMEM((planes, ny, nz), jnp.bfloat16),
        in_specs=[pl.BlockSpec(memory_space=pltpu.HBM), pl.BlockSpec(memory_space=pl.ANY)],
        out_specs=pl.BlockSpec(memory_space=pltpu.VMEM),
        scratch_shapes=[pltpu.VMEM((planes, ny, nz), jnp.float32), pltpu.SemaphoreType.DMA((planes,))],
        compiler_params=pltpu.CompilerParams(vmem_limit_bytes=2 * 1024 * 1024),
        cost_estimate=cost(1),
        name="rounded",
    )(in_hbm(fields), after)


def inner_kernel(run, *refs, ny, at):
    *refs, out, buffer, sems = refs
    snaps, fields = refs[:2], refs[2:]
    planes = snaps[0].shape[0]
    pieces, count = buffer.shape[0], buffer.shape[1]
    pairs = [(k, s) for k in range(pieces) for s in range(count)]
    copies = []
    for i in range(planes):
        for k in range(pieces):
            source = fields[k].at[(slice(None), *at[k], i)]
            copies.append(pltpu.make_async_copy(source, buffer.at[k, :, i], sems.at[i * pieces + k]))
    for copy in copies:
        copy.start()
    sums = tuple(jnp.zeros((8, 128), jnp.float32) for _ in range(2 * len(pairs)))
    for i in range(planes):
        for copy in copies[i * pieces : (i + 1) * pieces]:
            copy.wait()

        def body(t, sums, i=i):
            sums = list(sums)
            rows = pl.ds(pl.multiple_of(t * ROWS, ROWS), ROWS)
            for h in (0, 1):
                cols = pl.ds(h * 128, 128)
                mine = [snaps[j][i, rows, cols].astype(jnp.float32) for j in (0, 1)]
                for p, (k, s) in enumerate(pairs):
                    theirs = buffer[k, s, i, rows, cols].astype(jnp.float32)
                    for j in (0, 1):
                        both = mine[j] * theirs
                        sums[j * len(pairs) + p] = sums[j * len(pairs) + p] + (both[:8] + both[8:])
            return tuple(sums)

        sums = lax.fori_loop(0, ny // ROWS, body, sums, unroll=4)
    for j in (0, 1):
        for p, (k, s) in enumerate(pairs):
            out[j, (run[0] ^ k) * count + s] = sums[j * len(pairs) + p]


def inner(run, snaps, fields, at):
    planes, ny, nz = snaps[0].shape
    vmem, hbm = pl.BlockSpec(memory_space=pltpu.VMEM), pl.BlockSpec(memory_space=pltpu.HBM)
    count, pieces = fields[0].shape[0], len(fields)
    return pl.pallas_call(
        functools.partial(inner_kernel, ny=ny, at=at),
        out_shape=jax.ShapeDtypeStruct((2, count * pieces, 8, 128), jnp.float32),
        in_specs=[pl.BlockSpec(memory_space=pltpu.SMEM)] + [vmem] * 2 + [hbm] * pieces,
        out_specs=vmem,
        scratch_shapes=[
            pltpu.VMEM((pieces, count, planes, ny, nz), fields[0].dtype),
            pltpu.SemaphoreType.DMA((planes * pieces,)),
        ],
        compiler_params=pltpu.CompilerParams(vmem_limit_bytes=6 * 1024 * 1024),
        cost_estimate=cost(2),
        name="inner",
    )(run, *[in_vmem(a) for a in snaps], *[in_hbm(f) for f in fields])


def permute(array, axis, target):
    size = lax.axis_size(axis)
    return lax.ppermute(array, axis, [(i, target(i, size)) for i in range(size)])


def swap(array):
    return permute(array, "space", lambda i, n: i ^ 1)


def shift(array):
    return permute(array, "space", lambda i, n: (i + 2 - 4 * (i % 2)) % n)


def gather(snaps, c, near, runs):
    got, at = list(near), [(c,)] * len(near)
    half = runs // 2
    got.append(permute(snaps[:, c], "run", lambda i, n: i ^ half))
    bit = half // 2
    base = {half: got[-1]}
    while bit > 0:
        for k in list(base):
            base[k ^ bit] = permute(base[k], "run", lambda i, n: i ^ bit)
        bit //= 2
    return got[:half] + [base[k] for k in range(half, runs)], at + [()] * (runs - half)


def gather_near(snaps, runs):
    got = {0: snaps}
    bit = runs // 4
    while bit > 0:
        for k in list(got):
            got[k ^ bit] = permute(got[k], "run", lambda i, n: i ^ bit)
        bit //= 2
    return [got[k] for k in range(runs // 2)]


def on_device(adjoint_init, forward_snaps, base_speed, fwd_times, adj_times, horizon):
    runs, spaces = lax.axis_size("run"), lax.axis_size("space")
    _, parts, planes, ny, nz = adjoint_init.shape
    padded_speed = jnp.pad(base_speed, 1)
    shear_rate = 0.5 * (padded_speed[2:] - padded_speed[:-2])
    half = time_step * 0.5 * base_speed
    rows = jnp.stack([half + time_step * viscosity, time_step * viscosity - half, time_step * shear_rate])
    coefficients = jnp.broadcast_to(rows[:, :, None], (3, ny, 128))
    run = lax.axis_index("run").astype(jnp.int32)[None]
    odd = (lax.axis_index("space") % 2).astype(jnp.int32)[None]

    current = [(adjoint_init, (0, c)) for c in range(parts)]
    sent = []
    for c in range(parts):
        sent.append(rounded(adjoint_init, c, coefficients))
    fields, sums = [], [None] * (SNAP // 2)
    swapped, shifted = {}, {}
    for c in range(parts):
        swapped[0, c] = swap(sent[c])
    near = gather_near(forward_snaps, runs)
    for c in range(parts):
        fields.append(gather(forward_snaps, c, near, runs))
    for phase in range(SNAP // 2):
        kept = None
        for c in range(parts):
            if phase > 0:
                swapped[phase, c] = swap(sent[c])
            shifted[phase, c] = shift(swapped[phase, c])
            others = kept if c == 1 else None
            result = evolve(odd, coefficients, *current[c], swapped[phase, c], shifted[phase, c], others, keep=(c == 0))
            current[c], snaps = (result[0], ()), result[1:3]
            if c == 0:
                kept = result[3:]
            sent[c] = snaps[1]
            part = inner(run, snaps, *fields[c])
            sums[phase] = part if c == 0 else sums[phase] + part
    columns = jnp.stack(sums).reshape(SNAP, -1, 8, 128).sum(2)
    bit = 1
    while bit < spaces:
        columns = columns + permute(columns, "space", lambda i, n: i ^ bit)
        bit *= 2
    summed = columns.sum(-1)[None]
    scale = 1.0 / math.sqrt(parts * planes * spaces * ny * nz)
    inside = adj_times[:, :, None] + fwd_times[None, None, :] <= horizon[:, None, None]
    hankel = jnp.where(inside, summed * scale, jnp.zeros_like(summed))
    return (jnp.stack([q for q, _ in current])[None], hankel)


def solution(mesh):
    in_specs = (
        P("run", None, "space", None, None),
        P("run", None, "space", None, None),
        P(),
        P(),
        P("run", None),
        P("run"),
    )
    out_specs = (P("run", None, "space", None, None), P("run", None, None))
    return jax.shard_map(
        on_device, mesh=mesh, in_specs=in_specs, out_specs=out_specs, check_vma=False
    )
```

profile of v0, /device:TPU:0, one launch (start us, length us, event | category | flops | bytes accessed | tf_op | source)
XLA Modules:
  0.0 131.4 jit_solution(8881421027280722341)
XLA Ops:
  0.6 0.9 multiply_add_fusion
  1.6 1.3 rounded.5
  2.9 3.1 %collective-permute-start.8 = (bf16[4,192,256]{2,1,0:T(8,128)(2,1)S(1)}, bf16[4,192,256]{2,1,0:T(8,128)(2,1)S(1)}, u32[]{:S(2)}, u32[]{:S(2)}) collective-permute-start(bf16[4,192,256]{2,1,0:T(8,128)(2,1)S(1)} %rounded.5), channel_id=1, source_target_pairs={{0,1},{1,0},{2,3},{3,2},{4,5},{5,4},{6,7},{7,6},{8,9},{9,8},{10,11... | collective-permute-start | bytes 1179656 | tf_op jit(solution)/shard_map/ppermute | solution.py:232
  6.0 1.3 rounded.4
  7.3 1.3 rounded.3
  8.6 2.1 %collective-permute-start = (bf16[4,192,256]{2,1,0:T(8,128)(2,1)S(1)}, bf16[4,192,256]{2,1,0:T(8,128)(2,1)S(1)}, u32[]{:S(2)}, u32[]{:S(2)}) collective-permute-start(bf16[4,192,256]{2,1,0:T(8,128)(2,1)S(1)} %rounded.3), channel_id=1, source_target_pairs={{0,1},{1,0},{2,3},{3,2},{4,5},{5,4},{6,7},{7,6},{8,9},{9,8},{10,11... | collective-permute-start | bytes 1179656 | tf_op jit(solution)/shard_map/ppermute | solution.py:232
  10.7 5.3 %collective-permute-done.8.refs_3_ = bf16[4,192,256]{2,1,0:T(8,128)(2,1)S(1)} collective-permute-done((bf16[4,192,256]{2,1,0:T(8,128)(2,1)S(1)}, bf16[4,192,256]{2,1,0:T(8,128)(2,1)S(1)}, u32[]{:S(2)}, u32[]{:S(2)}) %collective-permute-start.8) | collective-permute-done | bytes 393248 | tf_op jit(solution)/shard_map/ppermute | solution.py:232
  16.0 2.1 %collective-permute-start.9 = (bf16[4,192,256]{2,1,0:T(8,128)(2,1)S(1)}, bf16[4,192,256]{2,1,0:T(8,128)(2,1)S(1)}, u32[]{:S(2)}, u32[]{:S(2)}) collective-permute-start(bf16[4,192,256]{2,1,0:T(8,128)(2,1)S(1)} %collective-permute-done.8.refs_3_), channel_id=1, source_target_pairs={{0,2},{1,7},{2,4},{3,1},{4,6},{5,3},{6,0},{7,5},{8,10},{9,15},{10,... | collective-permute-start | bytes 1179656 | tf_op jit(solution)/shard_map/ppermute | solution.py:232
  18.0 3.1 %slice_bitcast_fusion.1 = (bf16[2,4,192,256]{3,2,1,0:T(8,128)(2,1)}, bf16[2,4,192,256]{3,2,1,0:T(8,128)(2,1)}, bf16[2,4,192,256]{3,2,1,0:T(8,128)(2,1)}) fusion(bf16[2,3,4,192,256]{4,3,2,1,0:T(8,128)(2,1)} %refs_2_.17), kind=kLoop, calls=%fused_computation.2 | loop fusion | bytes 4718592 | tf_op jit(solution)/shard_map/squeeze | solution.py:246
  21.1 1.5 %collective-permute-start.17 = (bf16[2,4,192,256]{3,2,1,0:T(8,128)(2,1)}, bf16[2,4,192,256]{3,2,1,0:T(8,128)(2,1)}, u32[]{:S(2)}, u32[]{:S(2)}) collective-permute-start(bf16[2,4,192,256]{3,2,1,0:T(8,128)(2,1)} %get-tuple-element.56), channel_id=1, source_target_pairs={{0,16},{8,24},{16,0},{24,8},{1,17},{9,25},{17,1},{25,9},{2,18},{10... | collective-permute-start | bytes 2359304 | tf_op jit(solution)/shard_map/ppermute | solution.py:232
  22.6 1.8 %collective-permute-done.4.refs_3_ = bf16[4,192,256]{2,1,0:T(8,128)(2,1)S(1)} collective-permute-done((bf16[4,192,256]{2,1,0:T(8,128)(2,1)S(1)}, bf16[4,192,256]{2,1,0:T(8,128)(2,1)S(1)}, u32[]{:S(2)}, u32[]{:S(2)}) %collective-permute-start.4) | collective-permute-done | bytes 393248 | tf_op jit(solution)/shard_map/ppermute | solution.py:232
  24.4 2.1 %collective-permute-start.5 = (bf16[4,192,256]{2,1,0:T(8,128)(2,1)S(1)}, bf16[4,192,256]{2,1,0:T(8,128)(2,1)S(1)}, u32[]{:S(2)}, u32[]{:S(2)}) collective-permute-start(bf16[4,192,256]{2,1,0:T(8,128)(2,1)S(1)} %collective-permute-done.4.refs_3_), channel_id=1, source_target_pairs={{0,2},{1,7},{2,4},{3,1},{4,6},{5,3},{6,0},{7,5},{8,10},{9,15},{10,... | collective-permute-start | bytes 1179656 | tf_op jit(solution)/shard_map/ppermute | solution.py:232
  26.5 5.5 %collective-permute-done.refs_3_ = bf16[4,192,256]{2,1,0:T(8,128)(2,1)S(1)} collective-permute-done((bf16[4,192,256]{2,1,0:T(8,128)(2,1)S(1)}, bf16[4,192,256]{2,1,0:T(8,128)(2,1)S(1)}, u32[]{:S(2)}, u32[]{:S(2)}) %collective-permute-start) | collective-permute-done | bytes 393248 | tf_op jit(solution)/shard_map/ppermute | solution.py:232
  32.0 1.7 %collective-permute-start.13 = (bf16[2,4,192,256]{3,2,1,0:T(8,128)(2,1)}, bf16[2,4,192,256]{3,2,1,0:T(8,128)(2,1)}, u32[]{:S(2)}, u32[]{:S(2)}) collective-permute-start(bf16[2,4,192,256]{3,2,1,0:T(8,128)(2,1)} %get-tuple-element.55), channel_id=1, source_target_pairs={{0,16},{8,24},{16,0},{24,8},{1,17},{9,25},{17,1},{25,9},{2,18},{10... | collective-permute-start | bytes 2359304 | tf_op jit(solution)/shard_map/ppermute | solution.py:232
  33.7 0.8 copy-done.22
  34.4 1.6 %collective-permute-start.1 = (bf16[4,192,256]{2,1,0:T(8,128)(2,1)S(1)}, bf16[4,192,256]{2,1,0:T(8,128)(2,1)}, u32[]{:S(2)}, u32[]{:S(2)}) collective-permute-start(bf16[4,192,256]{2,1,0:T(8,128)(2,1)S(1)} %collective-permute-done.refs_3_), channel_id=1, source_target_pairs={{0,2},{1,7},{2,4},{3,1},{4,6},{5,3},{6,0},{7,5},{8,10},{9,15},{10,... | collective-permute-start | bytes 1179656 | tf_op jit(solution)/shard_map/ppermute | solution.py:232
  36.0 1.1 collective-permute-start.15
  37.1 1.0 copy-done.23
  38.1 4.7 %evolve_w.2 = (f32[4,192,256]{2,1,0:T(8,128)S(1)}, bf16[4,192,256]{2,1,0:T(8,128)(2,1)S(1)}, bf16[4,192,256]{2,1,0:T(8,128)(2,1)S(1)}) custom-call(s32[1]{0:T(128)} %bitcast.refs_0_, f32[3,192,128]{2,1,0:T(8,128)S(1)} %broadcast_in_dim.11.after.refs_1_, f32[1,3,4,192,256]{4,3,2,1,0:T(8,128)} %refs_2_.11, ...), custom_call_target="tpu_custom_call" | custom-call | bytes 13500000 | tf_op jit(solution)/shard_map/evolve_w/pallas_call | solution.py:136
  42.8 3.4 %collective-permute-done.1.refs_4_ = bf16[4,192,256]{2,1,0:T(8,128)(2,1)} collective-permute-done((bf16[4,192,256]{2,1,0:T(8,128)(2,1)S(1)}, bf16[4,192,256]{2,1,0:T(8,128)(2,1)}, u32[]{:S(2)}, u32[]{:S(2)}) %collective-permute-start.1) | collective-permute-done | bytes 393248 | tf_op jit(solution)/shard_map/ppermute | solution.py:232
  46.9 1.0 copy-done.21
  47.9 5.9 %evolve_u.2 = (f32[4,192,256]{2,1,0:T(8,128)S(1)}, bf16[4,192,256]{2,1,0:T(8,128)(2,1)S(1)}, bf16[4,192,256]{2,1,0:T(8,128)(2,1)S(1)}, f32[12,2,208,128]{3,2,1,0...) custom-call(s32[1]{0:T(128)} %bitcast.refs_0_, ...), custom_call_target="tpu_custom_call" | custom-call | bytes 13500000 | tf_op jit(solution)/shard_map/evolve_u/pallas_call | solution.py:136
  54.6 1.4 %collective-permute-start.2 = (bf16[4,192,256]{2,1,0:T(8,128)(2,1)S(1)}, bf16[4,192,256]{2,1,0:T(8,128)(2,1)S(1)}, u32[]{:S(2)}, u32[]{:S(2)}) collective-permute-start(bf16[4,192,256]{2,1,0:T(8,128)(2,1)S(1)} %get-tuple-element.29.refs_1_), channel_id=1, source_target_pairs={{0,1},{1,0},{2,3},{3,2},{4,5},{5,4},{6,7},{7,6},{8,9},{9,8},{10,11... | collective-permute-start | bytes 1179656 | tf_op jit(solution)/shard_map/ppermute | solution.py:232
  55.9 1.0 copy-done.11
  56.9 5.1 %evolve_v.2 = (f32[4,192,256]{2,1,0:T(8,128)S(1)}, bf16[4,192,256]{2,1,0:T(8,128)(2,1)S(1)}, bf16[4,192,256]{2,1,0:T(8,128)(2,1)S(1)}) custom-call(s32[1]{0:T(128)} %bitcast.refs_0_, f32[3,192,128]{2,1,0:T(8,128)S(1)} %broadcast_in_dim.11.after.refs_1_, f32[1,3,4,192,256]{4,3,2,1,0:T(8,128)} %refs_2_.11, bf16[4,192,256]{2,1,0:T(8,128)(2,1)S(1)} %copy-done.9, ...), custom_call_target="tpu_custom_call" | custom-call | bytes 13500000 | tf_op jit(solution)/shard_map/evolve_v/pallas_call | solution.py:136
  63.5 0.8 copy-done.6
  65.6 1.6 %collective-permute-start.3 = (bf16[4,192,256]{2,1,0:T(8,128)(2,1)S(1)}, bf16[4,192,256]{2,1,0:T(8,128)(2,1)S(1)}, u32[]{:S(2)}, u32[]{:S(2)}) collective-permute-start(bf16[4,192,256]{2,1,0:T(8,128)(2,1)S(1)} %collective-permute-done.2.refs_3_), channel_id=1, source_target_pairs={{0,2},{1,7},{2,4},{3,1},{4,6},{5,3},{6,0},{7,5},{8,10},{9,15},{10,... | collective-permute-start | bytes 1179656 | tf_op jit(solution)/shard_map/ppermute | solution.py:232
  68.0 4.2 %collective-permute-done.15.refs_4_ = bf16[2,4,192,256]{3,2,1,0:T(8,128)(2,1)} collective-permute-done((bf16[2,4,192,256]{3,2,1,0:T(8,128)(2,1)}, bf16[2,4,192,256]{3,2,1,0:T(8,128)(2,1)}, u32[]{:S(2)}, u32[]{:S(2)}) %collective-permute-start.15) | collective-permute-done | bytes 786464 | tf_op jit(solution)/shard_map/ppermute | solution.py:232
  72.6 6.0 %collective-permute-done.11.refs_4_ = bf16[4,192,256]{2,1,0:T(8,128)(2,1)S(1)} collective-permute-done((bf16[4,192,256]{2,1,0:T(8,128)(2,1)S(1)}, bf16[4,192,256]{2,1,0:T(8,128)(2,1)S(1)}, u32[]{:S(2)}, u32[]{:S(2)}) %collective-permute-start.11) | collective-permute-done | bytes 393248 | tf_op jit(solution)/shard_map/ppermute | solution.py:232
  79.4 4.1 %collective-permute-done.3.refs_4_ = bf16[4,192,256]{2,1,0:T(8,128)(2,1)S(1)} collective-permute-done((bf16[4,192,256]{2,1,0:T(8,128)(2,1)S(1)}, bf16[4,192,256]{2,1,0:T(8,128)(2,1)S(1)}, u32[]{:S(2)}, u32[]{:S(2)}) %collective-permute-start.3) | collective-permute-done | bytes 393248 | tf_op jit(solution)/shard_map/ppermute | solution.py:232
  84.3 1.0 copy-done.13
  85.3 1.0 copy-done.19
  86.2 3.7 %evolve_w.3 = (f32[4,192,256]{2,1,0:T(8,128)S(1)}, bf16[4,192,256]{2,1,0:T(8,128)(2,1)S(1)}, bf16[4,192,256]{2,1,0:T(8,128)(2,1)S(1)}) custom-call(s32[1]{0:T(128)} %bitcast.refs_0_, f32[3,192,128]{2,1,0:T(8,128)S(1)} %broadcast_in_dim.11.after.refs_1_, f32[4,192,256]{2,1,0:T(8,128)S(1)} %get-tuple-element.42.refs_2_, bf16[4,192,256]{2,1,0:T(8,128)(2,1)S(1)} %copy-done.13, ...), custom_call_target="tpu_custom_call" | custom-call | bytes 13500000 | tf_op jit(solution)/shard_map/evolve_w/pallas_call | solution.py:136
  90.0 1.0 copy-done.15
  91.0 1.0 copy-done.17
  92.0 3.8 %evolve_u.3 = (f32[4,192,256]{2,1,0:T(8,128)S(1)}, bf16[4,192,256]{2,1,0:T(8,128)(2,1)S(1)}, bf16[4,192,256]{2,1,0:T(8,128)(2,1)S(1)}, f32[12,2,208,128]{3,2,1,0...) custom-call(s32[1]{0:T(128)} %bitcast.refs_0_, ...), custom_call_target="tpu_custom_call" | custom-call | bytes 13500000 | tf_op jit(solution)/shard_map/evolve_u/pallas_call | solution.py:136
  95.8 5.2 %evolve_v.3 = (f32[4,192,256]{2,1,0:T(8,128)S(1)}, bf16[4,192,256]{2,1,0:T(8,128)(2,1)S(1)}, bf16[4,192,256]{2,1,0:T(8,128)(2,1)S(1)}) custom-call(s32[1]{0:T(128)} %bitcast.refs_0_, f32[3,192,128]{2,1,0:T(8,128)S(1)} %broadcast_in_dim.11.after.refs_1_, f32[4,192,256]{2,1,0:T(8,128)S(1)} %get-tuple-element.35.refs_2_, ...), custom_call_target="tpu_custom_call" | custom-call | bytes 13500000 | tf_op jit(solution)/shard_map/evolve_v/pallas_call | solution.py:136
  101.1 2.5 %inner.11 = f32[2,8,8,128]{3,2,1,0:T(8,128)S(1)} custom-call(s32[1]{0:T(128)} %bitcast.10.run, bf16[4,192,256]{2,1,0:T(8,128)(2,1)S(1)} %get-tuple-element.52.refs_0_, bf16[4,192,256]{2,1,0:T(8,128)(2,1)S(1)} %get-tuple-element.53.refs_1_, bf16[2,3,4,192,256]{4,3,2,1,0:T(8,128)(2,1)} %refs_2_.17, ...), custom_call_target="tpu_custom_call" | custom-call | bytes 6000000 | tf_op jit(solution)/shard_map/inner/pallas_call | solution.py:215
  103.6 2.5 %inner.9 = f32[2,8,8,128]{3,2,1,0:T(8,128)S(1)} custom-call(s32[1]{0:T(128)} %bitcast.10.run, bf16[4,192,256]{2,1,0:T(8,128)(2,1)S(1)} %get-tuple-element.48.refs_0_, bf16[4,192,256]{2,1,0:T(8,128)(2,1)S(1)} %get-tuple-element.49.refs_1_, bf16[2,3,4,192,256]{4,3,2,1,0:T(8,128)(2,1)} %refs_2_.17, ...), custom_call_target="tpu_custom_call" | custom-call | bytes 6000000 | tf_op jit(solution)/shard_map/inner/pallas_call | solution.py:215
  106.1 2.5 %inner.10 = f32[2,8,8,128]{3,2,1,0:T(8,128)S(1)} custom-call(s32[1]{0:T(128)} %bitcast.10.run, bf16[4,192,256]{2,1,0:T(8,128)(2,1)S(1)} %get-tuple-element.50.refs_0_, bf16[4,192,256]{2,1,0:T(8,128)(2,1)S(1)} %get-tuple-element.51.refs_1_, bf16[2,3,4,192,256]{4,3,2,1,0:T(8,128)(2,1)} %refs_2_.17, ...), custom_call_target="tpu_custom_call" | custom-call | bytes 6000000 | tf_op jit(solution)/shard_map/inner/pallas_call | solution.py:215
  108.7 2.6 %inner.8 = f32[2,8,8,128]{3,2,1,0:T(8,128)S(1)} custom-call(s32[1]{0:T(128)} %bitcast.10.run, bf16[4,192,256]{2,1,0:T(8,128)(2,1)S(1)} %get-tuple-element.47.refs_0_, bf16[4,192,256]{2,1,0:T(8,128)(2,1)S(1)} %get-tuple-element.43.refs_1_, bf16[2,3,4,192,256]{4,3,2,1,0:T(8,128)(2,1)} %refs_2_.17, ...), custom_call_target="tpu_custom_call" | custom-call | bytes 6000000 | tf_op jit(solution)/shard_map/inner/pallas_call | solution.py:215
  111.3 2.6 %inner.6 = f32[2,8,8,128]{3,2,1,0:T(8,128)S(1)} custom-call(s32[1]{0:T(128)} %bitcast.10.run, bf16[4,192,256]{2,1,0:T(8,128)(2,1)S(1)} %copy-done.1, bf16[4,192,256]{2,1,0:T(8,128)(2,1)S(1)} %copy-done.3, bf16[2,3,4,192,256]{4,3,2,1,0:T(8,128)(2,1)} %refs_2_.17, bf16[2,3,4,192,256]{4,3,2,1,0:T(8,128)(2,1)} %collective-permute-done.12.refs_3_, ...), custom_call_target="tpu_custom_call" | custom-call | bytes 6000000 | tf_op jit(solution)/shard_map/inner/pallas_call | solution.py:215
  113.9 2.5 %inner.7 = f32[2,8,8,128]{3,2,1,0:T(8,128)S(1)} custom-call(s32[1]{0:T(128)} %bitcast.10.run, bf16[4,192,256]{2,1,0:T(8,128)(2,1)S(1)} %copy-done.5, bf16[4,192,256]{2,1,0:T(8,128)(2,1)S(1)} %copy-done.7, bf16[2,3,4,192,256]{4,3,2,1,0:T(8,128)(2,1)} %refs_2_.17, bf16[2,3,4,192,256]{4,3,2,1,0:T(8,128)(2,1)} %collective-permute-done.12.refs_3_, ...), custom_call_target="tpu_custom_call" | custom-call | bytes 6000000 | tf_op jit(solution)/shard_map/inner/pallas_call | solution.py:215
  116.5 4.0 %collective-permute-start.19 = (f32[4,8,128]{2,1,0:T(8,128)S(1)}, f32[4,8,128]{2,1,0:T(8,128)S(1)}, u32[]{:S(2)}, u32[]{:S(2)}) collective-permute-start(f32[4,8,128]{2,1,0:T(8,128)S(1)} %bitcast.36), channel_id=1, source_target_pairs={{0,1},{1,0},{2,3},{3,2},{4,5},{5,4},{6,7},{7,6},{8,9},{9,8},{10,11... | collective-permute-start | bytes 49160 | tf_op jit(solution)/shard_map/ppermute | solution.py:232
  120.5 1.7 %collective-permute-done.19 = f32[4,8,128]{2,1,0:T(8,128)S(1)} collective-permute-done((f32[4,8,128]{2,1,0:T(8,128)S(1)}, f32[4,8,128]{2,1,0:T(8,128)S(1)}, u32[]{:S(2)}, u32[]{:S(2)}) %collective-permute-start.19) | collective-permute-done | bytes 16416 | tf_op jit(solution)/shard_map/ppermute | solution.py:232
  122.9 3.1 %collective-permute-done.20 = f32[4,8,128]{2,1,0:T(8,128)S(1)} collective-permute-done((f32[4,8,128]{2,1,0:T(8,128)S(1)}, f32[4,8,128]{2,1,0:T(8,128)S(1)}, u32[]{:S(2)}, u32[]{:S(2)}) %collective-permute-start.20) | collective-permute-done | bytes 16416 | tf_op jit(solution)/shard_map/ppermute | solution.py:232
  126.4 1.6 %maximum_bitcast_fusion = f32[1,3,4,192,256]{4,3,2,1,0:T(8,128)} fusion(f32[1,4,192,256]{3,2,1,0:T(8,128)S(1)} %bitcast.33, f32[1,4,192,256]{3,2,1,0:T(8,128)S(1)} %bitcast.35, f32[1,4,192,256]{3,2,1,0:T(8,128)S(1)} %bitcast.34), kind=kLoop, calls=%fused_computation | loop fusion | flops 1179648 | bytes 4718592 | tf_op jit(solution)/shard_map/broadcast_in_dim | solution.py:311
  128.0 2.7 %collective-permute-done.21 = f32[4,8,128]{2,1,0:T(8,128)S(1)} collective-permute-done((f32[4,8,128]{2,1,0:T(8,128)S(1)}, f32[4,8,128]{2,1,0:T(8,128)S(1)}, u32[]{:S(2)}, u32[]{:S(2)}) %collective-permute-start.21) | collective-permute-done | bytes 16416 | tf_op jit(solution)/shard_map/ppermute | solution.py:232
  (75 shorter events, 8.5 us)
Async XLA Ops:
  2.9 13.0 %collective-permute-start.8 = (bf16[4,192,256]{2,1,0:T(8,128)(2,1)S(1)}, bf16[4,192,256]{2,1,0:T(8,128)(2,1)S(1)}, u32[]{:S(2)}, u32[]{:S(2)}) collective-permute-start(bf16[4,192,256]{2,1,0:T(8,128)(2,1)S(1)} %rounded.5), channel_id=1, source_target_pairs={{0,1},{1,0},{2,3},{3,2},{4,5},{5,4},{6,7},{7,6},{8,9},{9,8},{10,11... | collective-permute-start | bytes 1179656 | tf_op jit(solution)/shard_map/ppermute | solution.py:232
  7.3 17.1 %collective-permute-start.4 = (bf16[4,192,256]{2,1,0:T(8,128)(2,1)S(1)}, bf16[4,192,256]{2,1,0:T(8,128)(2,1)S(1)}, u32[]{:S(2)}, u32[]{:S(2)}) collective-permute-start(bf16[4,192,256]{2,1,0:T(8,128)(2,1)S(1)} %rounded.4), channel_id=1, source_target_pairs={{0,1},{1,0},{2,3},{3,2},{4,5},{5,4},{6,7},{7,6},{8,9},{9,8},{10,11... | collective-permute-start | bytes 1179656 | tf_op jit(solution)/shard_map/ppermute | solution.py:232
  8.6 23.3 %collective-permute-start = (bf16[4,192,256]{2,1,0:T(8,128)(2,1)S(1)}, bf16[4,192,256]{2,1,0:T(8,128)(2,1)S(1)}, u32[]{:S(2)}, u32[]{:S(2)}) collective-permute-start(bf16[4,192,256]{2,1,0:T(8,128)(2,1)S(1)} %rounded.3), channel_id=1, source_target_pairs={{0,1},{1,0},{2,3},{3,2},{4,5},{5,4},{6,7},{7,6},{8,9},{9,8},{10,11... | collective-permute-start | bytes 1179656 | tf_op jit(solution)/shard_map/ppermute | solution.py:232
  10.7 90.4 %collective-permute-start.12 = (bf16[2,3,4,192,256]{4,3,2,1,0:T(8,128)(2,1)}, bf16[2,3,4,192,256]{4,3,2,1,0:T(8,128)(2,1)}, u32[]{:S(2)}, u32[]{:S(2)}) collective-permute-start(bf16[2,3,4,192,256]{4,3,2,1,0:T(8,128)(2,1)} %refs_2_.17), channel_id=1, source_target_pairs={{0,8},{8,0},{16,24},{24,16},{1,9},{9,1},{17,25},{25,17},{2,10},{10... | collective-permute-start | bytes 7077896 | tf_op jit(solution)/shard_map/ppermute | solution.py:232
  16.0 17.7 %collective-permute-start.9 = (bf16[4,192,256]{2,1,0:T(8,128)(2,1)S(1)}, bf16[4,192,256]{2,1,0:T(8,128)(2,1)S(1)}, u32[]{:S(2)}, u32[]{:S(2)}) collective-permute-start(bf16[4,192,256]{2,1,0:T(8,128)(2,1)S(1)} %collective-permute-done.8.refs_3_), channel_id=1, source_target_pairs={{0,2},{1,7},{2,4},{3,1},{4,6},{5,3},{6,0},{7,5},{8,10},{9,15},{10,... | collective-permute-start | bytes 1179656 | tf_op jit(solution)/shard_map/ppermute | solution.py:232
  21.1 33.5 %collective-permute-start.17 = (bf16[2,4,192,256]{3,2,1,0:T(8,128)(2,1)}, bf16[2,4,192,256]{3,2,1,0:T(8,128)(2,1)}, u32[]{:S(2)}, u32[]{:S(2)}) collective-permute-start(bf16[2,4,192,256]{3,2,1,0:T(8,128)(2,1)} %get-tuple-element.56), channel_id=1, source_target_pairs={{0,16},{8,24},{16,0},{24,8},{1,17},{9,25},{17,1},{25,9},{2,18},{10... | collective-permute-start | bytes 2359304 | tf_op jit(solution)/shard_map/ppermute | solution.py:232
  24.4 21.9 %copy-start.8 = (bf16[4,192,256]{2,1,0:T(8,128)(2,1)}, bf16[4,192,256]{2,1,0:T(8,128)(2,1)S(1)}, u32[]{:S(2)}) copy-start(bf16[4,192,256]{2,1,0:T(8,128)(2,1)S(1)} %collective-permute-done.4.refs_3_) | copy-start | bytes 1179652
  24.4 11.6 %collective-permute-start.5 = (bf16[4,192,256]{2,1,0:T(8,128)(2,1)S(1)}, bf16[4,192,256]{2,1,0:T(8,128)(2,1)S(1)}, u32[]{:S(2)}, u32[]{:S(2)}) collective-permute-start(bf16[4,192,256]{2,1,0:T(8,128)(2,1)S(1)} %collective-permute-done.4.refs_3_), channel_id=1, source_target_pairs={{0,2},{1,7},{2,4},{3,1},{4,6},{5,3},{6,0},{7,5},{8,10},{9,15},{10,... | collective-permute-start | bytes 1179656 | tf_op jit(solution)/shard_map/ppermute | solution.py:232
  32.0 14.3 %copy-start.20 = (bf16[4,192,256]{2,1,0:T(8,128)(2,1)}, bf16[4,192,256]{2,1,0:T(8,128)(2,1)S(1)}, u32[]{:S(2)}) copy-start(bf16[4,192,256]{2,1,0:T(8,128)(2,1)S(1)} %collective-permute-done.refs_3_) | copy-start | bytes 1179652
  32.0 30.9 %collective-permute-start.13 = (bf16[2,4,192,256]{3,2,1,0:T(8,128)(2,1)}, bf16[2,4,192,256]{3,2,1,0:T(8,128)(2,1)}, u32[]{:S(2)}, u32[]{:S(2)}) collective-permute-start(bf16[2,4,192,256]{3,2,1,0:T(8,128)(2,1)} %get-tuple-element.55), channel_id=1, source_target_pairs={{0,16},{8,24},{16,0},{24,8},{1,17},{9,25},{17,1},{25,9},{2,18},{10... | collective-permute-start | bytes 2359304 | tf_op jit(solution)/shard_map/ppermute | solution.py:232
  33.7 0.8 copy-start.22
  34.4 11.8 %collective-permute-start.1 = (bf16[4,192,256]{2,1,0:T(8,128)(2,1)S(1)}, bf16[4,192,256]{2,1,0:T(8,128)(2,1)}, u32[]{:S(2)}, u32[]{:S(2)}) collective-permute-start(bf16[4,192,256]{2,1,0:T(8,128)(2,1)S(1)} %collective-permute-done.refs_3_), channel_id=1, source_target_pairs={{0,2},{1,7},{2,4},{3,1},{4,6},{5,3},{6,0},{7,5},{8,10},{9,15},{10,... | collective-permute-start | bytes 1179656 | tf_op jit(solution)/shard_map/ppermute | solution.py:232
  36.0 17.8 %copy-start.10 = (bf16[4,192,256]{2,1,0:T(8,128)(2,1)}, bf16[4,192,256]{2,1,0:T(8,128)(2,1)S(1)}, u32[]{:S(2)}) copy-start(bf16[4,192,256]{2,1,0:T(8,128)(2,1)S(1)} %collective-permute-done.5.refs_4_) | copy-start | bytes 1179652
  36.0 36.1 %collective-permute-start.15 = (bf16[2,4,192,256]{3,2,1,0:T(8,128)(2,1)}, bf16[2,4,192,256]{3,2,1,0:T(8,128)(2,1)}, u32[]{:S(2)}, u32[]{:S(2)}) collective-permute-start(bf16[2,4,192,256]{3,2,1,0:T(8,128)(2,1)} %get-tuple-element.54), channel_id=1, source_target_pairs={{0,16},{8,24},{16,0},{24,8},{1,17},{9,25},{17,1},{25,9},{2,18},{10... | collective-permute-start | bytes 2359304 | tf_op jit(solution)/shard_map/ppermute | solution.py:232
  37.1 1.0 copy-start.23
  46.2 18.1 %collective-permute-start.10 = (bf16[4,192,256]{2,1,0:T(8,128)(2,1)S(1)}, bf16[4,192,256]{2,1,0:T(8,128)(2,1)S(1)}, u32[]{:S(2)}, u32[]{:S(2)}) collective-permute-start(bf16[4,192,256]{2,1,0:T(8,128)(2,1)S(1)} %get-tuple-element.43.refs_1_), channel_id=1, source_target_pairs={{0,1},{1,0},{2,3},{3,2},{4,5},{5,4},{6,7},{7,6},{8,9},{9,8},{10,11... | collective-permute-start | bytes 1179656 | tf_op jit(solution)/shard_map/ppermute | solution.py:232
  46.9 1.0 copy-start.21
  47.9 8.0 %copy-start.9 = (bf16[4,192,256]{2,1,0:T(8,128)(2,1)S(1)}, bf16[4,192,256]{2,1,0:T(8,128)(2,1)}, u32[]{:S(2)}) copy-start(bf16[4,192,256]{2,1,0:T(8,128)(2,1)} %copy-done.8) | copy-start | bytes 1179652
  53.8 0.8 copy-start
  54.6 7.5 %copy-start.2 = (bf16[4,192,256]{2,1,0:T(8,128)(2,1)}, bf16[4,192,256]{2,1,0:T(8,128)(2,1)S(1)}, u32[]{:S(2)}) copy-start(bf16[4,192,256]{2,1,0:T(8,128)(2,1)S(1)} %get-tuple-element.29.refs_1_) | copy-start | bytes 1179652
  54.6 11.0 %collective-permute-start.2 = (bf16[4,192,256]{2,1,0:T(8,128)(2,1)S(1)}, bf16[4,192,256]{2,1,0:T(8,128)(2,1)S(1)}, u32[]{:S(2)}, u32[]{:S(2)}) collective-permute-start(bf16[4,192,256]{2,1,0:T(8,128)(2,1)S(1)} %get-tuple-element.29.refs_1_), channel_id=1, source_target_pairs={{0,1},{1,0},{2,3},{3,2},{4,5},{5,4},{6,7},{7,6},{8,9},{9,8},{10,11... | collective-permute-start | bytes 1179656 | tf_op jit(solution)/shard_map/ppermute | solution.py:232
  55.9 1.0 copy-start.11
  62.0 0.8 copy-start.4
  62.8 9.4 %collective-permute-start.6 = (bf16[4,192,256]{2,1,0:T(8,128)(2,1)S(1)}, bf16[4,192,256]{2,1,0:T(8,128)(2,1)}, u32[]{:S(2)}, u32[]{:S(2)}) collective-permute-start(bf16[4,192,256]{2,1,0:T(8,128)(2,1)S(1)} %get-tuple-element.36.refs_1_), channel_id=1, source_target_pairs={{0,1},{1,0},{2,3},{3,2},{4,5},{5,4},{6,7},{7,6},{8,9},{9,8},{10,11... | collective-permute-start | bytes 1179656 | tf_op jit(solution)/shard_map/ppermute | solution.py:232
  63.5 0.8 copy-start.6
  64.3 14.3 %collective-permute-start.11 = (bf16[4,192,256]{2,1,0:T(8,128)(2,1)S(1)}, bf16[4,192,256]{2,1,0:T(8,128)(2,1)S(1)}, u32[]{:S(2)}, u32[]{:S(2)}) collective-permute-start(bf16[4,192,256]{2,1,0:T(8,128)(2,1)S(1)} %collective-permute-done.10.refs_3_), channel_id=1, source_target_pairs={{0,2},{1,7},{2,4},{3,1},{4,6},{5,3},{6,0},{7,5},{8,10},{9,15},{10,... | collective-permute-start | bytes 1179656 | tf_op jit(solution)/shard_map/ppermute | solution.py:232
  64.8 0.8 copy-start.12
  65.6 17.9 %collective-permute-start.3 = (bf16[4,192,256]{2,1,0:T(8,128)(2,1)S(1)}, bf16[4,192,256]{2,1,0:T(8,128)(2,1)S(1)}, u32[]{:S(2)}, u32[]{:S(2)}) collective-permute-start(bf16[4,192,256]{2,1,0:T(8,128)(2,1)S(1)} %collective-permute-done.2.refs_3_), channel_id=1, source_target_pairs={{0,2},{1,7},{2,4},{3,1},{4,6},{5,3},{6,0},{7,5},{8,10},{9,15},{10,... | collective-permute-start | bytes 1179656 | tf_op jit(solution)/shard_map/ppermute | solution.py:232
  67.2 0.8 copy-start.14
  72.1 28.9 %collective-permute-start.18 = (bf16[2,4,192,256]{3,2,1,0:T(8,128)(2,1)}, bf16[2,4,192,256]{3,2,1,0:T(8,128)(2,1)}, u32[]{:S(2)}, u32[]{:S(2)}) collective-permute-start(bf16[2,4,192,256]{3,2,1,0:T(8,128)(2,1)} %collective-permute-done.17.refs_4_), channel_id=1, source_target_pairs={{0,8},{8,0},{16,24},{24,16},{1,9},{9,1},{17,25},{25,17},{2,10},{10... | collective-permute-start | bytes 2359304 | tf_op jit(solution)/shard_map/ppermute | solution.py:232
  72.2 31.4 %collective-permute-start.14 = (bf16[2,4,192,256]{3,2,1,0:T(8,128)(2,1)}, bf16[2,4,192,256]{3,2,1,0:T(8,128)(2,1)}, u32[]{:S(2)}, u32[]{:S(2)}) collective-permute-start(bf16[2,4,192,256]{3,2,1,0:T(8,128)(2,1)} %collective-permute-done.13.refs_4_), channel_id=1, source_target_pairs={{0,8},{8,0},{16,24},{24,16},{1,9},{9,1},{17,25},{25,17},{2,10},{10... | collective-permute-start | bytes 2359304 | tf_op jit(solution)/shard_map/ppermute | solution.py:232
  78.6 0.7 copy-start.18
  79.4 26.8 %collective-permute-start.16 = (bf16[2,4,192,256]{3,2,1,0:T(8,128)(2,1)}, bf16[2,4,192,256]{3,2,1,0:T(8,128)(2,1)}, u32[]{:S(2)}, u32[]{:S(2)}) collective-permute-start(bf16[2,4,192,256]{3,2,1,0:T(8,128)(2,1)} %collective-permute-done.15.refs_4_), channel_id=1, source_target_pairs={{0,8},{8,0},{16,24},{24,16},{1,9},{9,1},{17,25},{25,17},{2,10},{10... | collective-permute-start | bytes 2359304 | tf_op jit(solution)/shard_map/ppermute | solution.py:232
  83.5 0.8 copy-start.16
  84.3 11.6 %collective-permute-start.7 = (bf16[4,192,256]{2,1,0:T(8,128)(2,1)}, bf16[4,192,256]{2,1,0:T(8,128)(2,1)}, u32[]{:S(2)}, u32[]{:S(2)}) collective-permute-start(bf16[4,192,256]{2,1,0:T(8,128)(2,1)} %collective-permute-done.6.refs_3_), channel_id=1, source_target_pairs={{0,2},{1,7},{2,4},{3,1},{4,6},{5,3},{6,0},{7,5},{8,10},{9,15},{10,... | collective-permute-start | bytes 1179656 | tf_op jit(solution)/shard_map/ppermute | solution.py:232
  84.3 1.0 copy-start.13
  85.3 1.0 copy-start.19
  90.0 1.0 copy-start.15
  91.0 1.0 copy-start.17
  108.7 2.6 %copy-start.1 = (bf16[4,192,256]{2,1,0:T(8,128)(2,1)S(1)}, bf16[4,192,256]{2,1,0:T(8,128)(2,1)}, u32[]{:S(2)}) copy-start(bf16[4,192,256]{2,1,0:T(8,128)(2,1)} %copy-done) | copy-start | bytes 1179652
  108.7 2.6 %copy-start.3 = (bf16[4,192,256]{2,1,0:T(8,128)(2,1)S(1)}, bf16[4,192,256]{2,1,0:T(8,128)(2,1)}, u32[]{:S(2)}) copy-start(bf16[4,192,256]{2,1,0:T(8,128)(2,1)} %copy-done.2) | copy-start | bytes 1179652
  111.3 2.6 %copy-start.5 = (bf16[4,192,256]{2,1,0:T(8,128)(2,1)S(1)}, bf16[4,192,256]{2,1,0:T(8,128)(2,1)}, u32[]{:S(2)}) copy-start(bf16[4,192,256]{2,1,0:T(8,128)(2,1)} %copy-done.4) | copy-start | bytes 1179652
  111.3 2.6 %copy-start.7 = (bf16[4,192,256]{2,1,0:T(8,128)(2,1)S(1)}, bf16[4,192,256]{2,1,0:T(8,128)(2,1)}, u32[]{:S(2)}) copy-start(bf16[4,192,256]{2,1,0:T(8,128)(2,1)} %copy-done.6) | copy-start | bytes 1179652
  116.5 5.8 %collective-permute-start.19 = (f32[4,8,128]{2,1,0:T(8,128)S(1)}, f32[4,8,128]{2,1,0:T(8,128)S(1)}, u32[]{:S(2)}, u32[]{:S(2)}) collective-permute-start(f32[4,8,128]{2,1,0:T(8,128)S(1)} %bitcast.36), channel_id=1, source_target_pairs={{0,1},{1,0},{2,3},{3,2},{4,5},{5,4},{6,7},{7,6},{8,9},{9,8},{10,11... | collective-permute-start | bytes 49160 | tf_op jit(solution)/shard_map/ppermute | solution.py:232
  122.3 3.7 %collective-permute-start.20 = (f32[4,8,128]{2,1,0:T(8,128)S(1)}, f32[4,8,128]{2,1,0:T(8,128)S(1)}, u32[]{:S(2)}, u32[]{:S(2)}) collective-permute-start(f32[4,8,128]{2,1,0:T(8,128)S(1)} %bitcast_add_fusion), channel_id=1, source_target_pairs={{0,2},{1,3},{2,0},{3,1},{4,6},{5,7},{6,4},{7,5},{8,10},{9,11},{10,... | collective-permute-start | bytes 49160 | tf_op jit(solution)/shard_map/ppermute | solution.py:232
  126.0 4.6 %collective-permute-start.21 = (f32[4,8,128]{2,1,0:T(8,128)S(1)}, f32[4,8,128]{2,1,0:T(8,128)S(1)}, u32[]{:S(2)}, u32[]{:S(2)}) collective-permute-start(f32[4,8,128]{2,1,0:T(8,128)S(1)} %add.61), channel_id=1, source_target_pairs={{0,4},{1,5},{2,6},{3,7},{4,0},{5,1},{6,2},{7,3},{8,12},{9,13},{10,... | collective-permute-start | bytes 49160 | tf_op jit(solution)/shard_map/ppermute | solution.py:232
  126.4 4.3 %copy-start.24 = (s32[8]{0:T(128)S(1)}, s32[8]{0:T(128)}, u32[]{:S(2)}) copy-start(s32[8]{0:T(128)} %param.9) | copy-start | bytes 100
  126.4 4.3 %copy-start.25 = (s32[1,4]{1,0:T(1,128)S(1)}, s32[1,4]{1,0:T(1,128)}, u32[]{:S(2)}) copy-start(s32[1,4]{1,0:T(1,128)} %param.10) | copy-start | bytes 52
where the time goes:
time: 132 us; the launch traced here: 131 us
  Pallas kernels  47.5 us (36%)
  waiting for transfers between devices  37.8 us (29%)
  starting transfers between devices  24.9 us (19%)
  local copies, waits for them, and re-layouts  16.3 us (12%)
  other arithmetic  3.25 us (2%)
  between operations  1.62 us (1%)
    ppermute x22, waiting for transfers between devices, permute(): lax.ppermute(array, axis, [(i, target(i, size)) for i in range(size)])  37.8 us
    pallas_call x6, Pallas kernels, evolve(): pl.pallas_call(functools.partial(evolve_kernel, coupled=coupled, keep=kee...  28.5 us
    ppermute x22, starting transfers between devices, permute(): lax.ppermute(array, axis, [(i, target(i, size)) for i in range(size)])  24.9 us
    pallas_call x6, Pallas kernels, inner(): pl.pallas_call(functools.partial(inner_kernel, ny=ny, at=at), out_shape=j...  15.2 us
    unnamed x52, local copies, waits for them, and re-layouts  13.1 us
    pallas_call x3, Pallas kernels, rounded(): pl.pallas_call(functools.partial(round_kernel, c=c), out_shape=pltpu.VMEM...  3.79 us
    squeeze x1, local copies, waits for them, and re-layouts, gather(): got.append(permute(snaps[:, c], 'run', lambda i, n: i ^ half))  3.05 us
  transfers between devices with their start and end apart: 22, of which 11 were waited for; matrix products, arithmetic and copies ran while one was open for 4% of the time, Pallas kernels for 27%

commit v1 on v0

v1 whole, which is shorter than its diff:
```python
import functools
import math

import jax
import jax.numpy as jnp
from jax import lax
from jax.experimental import pallas as pl
from jax.experimental.pallas import tpu as pltpu
from jax.sharding import PartitionSpec as P

SNAP = 4
time_step = 0.5
viscosity = 0.2


PAD = 8
TILE = 16


def in_hbm(array):
    return pltpu.with_memory_space_constraint(array, pltpu.HBM)


def in_vmem(array):
    return pltpu.with_memory_space_constraint(array, pltpu.VMEM)


def cost(us):
    return pl.CostEstimate(flops=0, transcendentals=0, bytes_accessed=int(us * 3.0e6))


def evolve_kernel(*refs, coupled, planes, ny, at, pieces, split):
    refs = list(refs)
    coefficients, around_z = refs.pop(0), refs.pop(0)
    own = refs.pop(0)
    swapped, shifted = [refs.pop(0) for _ in range(pieces)], [refs.pop(0) for _ in range(pieces)]
    others = [refs.pop(0) for _ in range(4)] if coupled else [None] * 4
    new, snaps = refs.pop(0), [[refs.pop(0)], [refs.pop(0) for _ in range(split)]]
    work = [refs.pop(0) for _ in range(4)]
    sems = refs.pop(0)
    n = planes
    halves = [(h, pl.ds(h * 128, 128)) for h in (0, 1)]
    rows = pl.ds(PAD, ny)
    copies = []
    for i in range(n):
        for h, cols in halves:
            source = own.at[(*at, i, slice(None), cols)]
            copies.append(pltpu.make_async_copy(source, work[0].at[n + i, h, rows, :], sems.at[2 * i + h]))
    for copy in copies:
        copy.start()
    swap_at = jnp.where(lax.axis_index("space") % 2 == 1, 0, 2 * n)
    shift_at = 2 * n - swap_at
    zeros = jnp.zeros((PAD, 128), jnp.float32)
    for buffer in work:
        for i in range(buffer.shape[0]):
            for h in (0, 1):
                buffer[i, h, pl.ds(0, PAD), :] = zeros
                buffer[i, h, pl.ds(PAD + ny, PAD), :] = zeros
    for i in range(n):
        for h, cols in halves:
            piece, place = i * pieces // n, i % (n // pieces)
            work[0][swap_at + i, h, rows, :] = swapped[piece][place, :, cols].astype(jnp.float32)
            work[0][shift_at + i, h, rows, :] = shifted[piece][place, :, cols].astype(jnp.float32)
    for copy in copies:
        copy.wait()

    weight = time_step * viscosity
    for k in range(4):
        src = work[k]
        second = k % 2
        count = 3 * n - 2 - 2 * k
        lines = [jnp.concatenate([src[j, h, rows, :] for h in (0, 1)], axis=1) for j in range(1, 1 + count)]
        lines = jnp.concatenate([line.astype(jnp.bfloat16) for line in lines], axis=0)
        beside = jnp.dot(lines, around_z[...], preferred_element_type=jnp.float32)
        east, west, shear = coefficients[3 * second], coefficients[3 * second + 1], coefficients[3 * second + 2]
        for j in range(1, 1 + count):
            i = j + k
            for h, cols in halves:
                around = src[j, h, pl.ds(PAD + 1, ny), :] + src[j, h, pl.ds(PAD - 1, ny), :]
                around = around + beside[(j - 1) * ny : j * ny, h * 128 : (h + 1) * 128]
                centre = src[j, h, rows, :]
                if second:
                    got = (weight * weight) * around + (weight * (1.0 - 6.0 * weight)) * centre
                else:
                    got = around + ((1.0 - 6.0 * weight) / weight) * centre
                got = got + (east * src[j + 1, h, rows, :] + west * src[j - 1, h, rows, :])
                if coupled:
                    got = got - shear * others[k][j, h, rows, :]
                if second:
                    got = work[k - 1][j + 1, h, rows, :] + got
                if k < 3:
                    work[k + 1][j - 1, h, rows, :] = got
                if second and n <= i < 2 * n:
                    scaled = (0.5 if k == 1 else 0.25) * got
                    into = snaps[k // 2]
                    into[(i - n) * len(into) // n][i % (n // len(into)), :, cols] = scaled.astype(jnp.bfloat16)
                    if k == 3:
                        new[i - n, :, cols] = scaled


def evolve(coefficients, around_z, own, at, swapped, shifted, others=None, keep=False, split=1):
    pieces = len(swapped)
    planes, ny, nz = swapped[0].shape
    planes *= pieces
    coupled = others is not None
    vmem = pl.BlockSpec(memory_space=pltpu.VMEM)
    kept = [jax.ShapeDtypeStruct((3 * planes - 2 * k, 2, ny + 2 * PAD, 128), jnp.float32) for k in range(4)]
    first = len(at) > 0
    new = (pltpu.VMEM if first else jax.ShapeDtypeStruct)((planes, ny, nz), jnp.float32)
    work = [pltpu.VMEM(s.shape, s.dtype) for s in kept]
    scratch = [] if keep else work
    outs = [new] + [pltpu.VMEM((planes // k, ny, nz), jnp.bfloat16) for k in [1] + [split] * split] + (work if keep else [])
    before = [coefficients, around_z]
    after = [in_vmem(a) for a in swapped + shifted + (tuple(others) if coupled else ())]
    own = in_hbm(own) if first else in_vmem(own)
    return pl.pallas_call(
        functools.partial(evolve_kernel, coupled=coupled, planes=planes, ny=ny, at=at, pieces=pieces, split=split),
        out_shape=outs,
        in_specs=[vmem] * len(before)
        + [pl.BlockSpec(memory_space=pltpu.HBM) if first else vmem]
        + [vmem] * len(after),
        out_specs=[vmem] * len(outs),
        scratch_shapes=scratch + [pltpu.SemaphoreType.DMA((2 * planes,))],
        compiler_params=pltpu.CompilerParams(vmem_limit_bytes=12 * 1024 * 1024),
        cost_estimate=cost(4.5),
        name="evolve_v" if coupled else ("evolve_u" if keep else "evolve_w"),
    )(*before, own, *after)


def round_kernel(fields, snaps, *refs, c):
    *outs, chunk, buffer, sems, chunk_sems = refs
    planes = buffer.shape[0]
    copies = [pltpu.make_async_copy(fields.at[0, c, i], buffer.at[i], sems.at[i]) for i in range(planes)]
    slices = [pltpu.make_async_copy(snaps.at[s, c], chunk.at[s], chunk_sems.at[s]) for s in range(chunk.shape[0])]
    for copy in copies + slices:
        copy.start()
    for i, copy in enumerate(copies):
        copy.wait()
        outs[i * len(outs) // planes][i % (planes // len(outs))] = buffer[i].astype(jnp.bfloat16)
    for copy in slices:
        copy.wait()


def rounded(fields, snaps, c):
    _, _, planes, ny, nz = fields.shape
    count = snaps.shape[0]
    vmem, hbm = pl.BlockSpec(memory_space=pltpu.VMEM), pl.BlockSpec(memory_space=pltpu.HBM)
    half = pltpu.VMEM((planes // 2, ny, nz), jnp.bfloat16)
    return pl.pallas_call(
        functools.partial(round_kernel, c=c),
        out_shape=[half, half, pltpu.VMEM((count, planes, ny, nz), snaps.dtype)],
        in_specs=[hbm, hbm],
        out_specs=[vmem] * 3,
        scratch_shapes=[
            pltpu.VMEM((planes, ny, nz), jnp.float32),
            pltpu.SemaphoreType.DMA((planes,)),
            pltpu.SemaphoreType.DMA((count,)),
        ],
        compiler_params=pltpu.CompilerParams(vmem_limit_bytes=2 * 1024 * 1024),
        cost_estimate=cost(1),
        name="rounded",
    )(in_hbm(fields), in_hbm(snaps))


def prepare_kernel(fields, snaps, speed, *refs, planes, ny, nz):
    parts = fields.shape[1]
    outs, chunks = refs[: parts - 1], refs[parts - 1 : 2 * parts - 2]
    coefficients, around_z, buffer, padded, sems, chunk_sems = refs[2 * parts - 2 :]
    copies = []
    for c in range(1, parts):
        for i in range(planes):
            at = (c - 1) * planes + i
            copies.append(pltpu.make_async_copy(fields.at[0, c, i], buffer.at[c - 1, i], sems.at[at]))
    count = snaps.shape[0]
    slices = [
        pltpu.make_async_copy(snaps.at[s, c], chunks[c - 1].at[s], chunk_sems.at[(c - 1) * count + s])
        for c in range(1, parts)
        for s in range(count)
    ]
    for copy in copies + slices:
        copy.start()
    base = jnp.broadcast_to(speed[...], (128, ny)).T
    padded[pl.ds(0, PAD), :] = jnp.zeros((PAD, 128), jnp.float32)
    padded[pl.ds(PAD + ny, PAD), :] = jnp.zeros((PAD, 128), jnp.float32)
    padded[pl.ds(PAD, ny), :] = base
    shear = (0.5 * time_step) * (padded[pl.ds(PAD + 1, ny), :] - padded[pl.ds(PAD - 1, ny), :])
    weight = time_step * viscosity
    half = (0.5 * time_step) * base
    for k, scale in enumerate((1.0 / weight, weight)):
        coefficients[3 * k] = scale * (half + weight)
        coefficients[3 * k + 1] = scale * (weight - half)
        coefficients[3 * k + 2] = scale * shear
    apart = lax.broadcasted_iota(jnp.int32, (nz, nz), 0) - lax.broadcasted_iota(jnp.int32, (nz, nz), 1)
    apart = jnp.abs(apart)
    around_z[...] = jnp.where((apart == 1) | (apart == nz - 1), 1.0, 0.0).astype(jnp.bfloat16)
    for at, copy in enumerate(copies):
        copy.wait()
        c, i = at // planes, at % planes
        outs[c][i] = buffer[c, i].astype(jnp.bfloat16)
    for copy in slices:
        copy.wait()


def prepare(fields, snaps, speed):
    _, parts, planes, ny, nz = fields.shape
    count = snaps.shape[0]
    vmem, hbm = pl.BlockSpec(memory_space=pltpu.VMEM), pl.BlockSpec(memory_space=pltpu.HBM)
    outs = [pltpu.VMEM((planes, ny, nz), jnp.bfloat16)] * (parts - 1)
    outs += [pltpu.VMEM((count, planes, ny, nz), snaps.dtype)] * (parts - 1)
    outs += [pltpu.VMEM((6, ny, 128), jnp.float32), pltpu.VMEM((nz, nz), jnp.bfloat16)]
    got = pl.pallas_call(
        functools.partial(prepare_kernel, planes=planes, ny=ny, nz=nz),
        out_shape=outs,
        in_specs=[hbm, hbm, vmem],
        out_specs=[vmem] * len(outs),
        scratch_shapes=[
            pltpu.VMEM((parts - 1, planes, ny, nz), jnp.float32),
            pltpu.VMEM((ny + 2 * PAD, 128), jnp.float32),
            pltpu.SemaphoreType.DMA(((parts - 1) * planes,)),
            pltpu.SemaphoreType.DMA(((parts - 1) * count,)),
        ],
        compiler_params=pltpu.CompilerParams(vmem_limit_bytes=4 * 1024 * 1024),
        cost_estimate=cost(2),
        name="prepare",
    )(in_hbm(fields), in_hbm(snaps), speed[None])
    return got[: parts - 1], got[parts - 1 : 2 * parts - 2], got[-2], got[-1]


def inner_kernel(*refs, pieces, at):
    run = lax.axis_index("run")
    *refs, out = refs
    snaps, fields = [refs[0:1], refs[1 : 1 + pieces]], refs[1 + pieces :]
    count = fields[0].shape[0]
    planes, ny, _ = refs[0].shape
    pairs = [(k, s) for k in range(len(fields)) for s in range(count)]
    sums = tuple(jnp.zeros((8, 128), jnp.float32) for _ in range(2 * len(pairs)))
    for i in range(planes):

        def body(t, sums, i=i):
            sums = list(sums)
            rows = pl.ds(pl.multiple_of(t * TILE, TILE), TILE)
            for h in (0, 1):
                cols = pl.ds(h * 128, 128)
                mine = []
                for split in snaps:
                    piece, place = i * len(split) // planes, i % (planes // len(split))
                    mine.append(split[piece][place, rows, cols].astype(jnp.float32))
                for p, (k, s) in enumerate(pairs):
                    theirs = fields[k][(s, *at[k], i, rows, cols)].astype(jnp.float32)
                    for j in (0, 1):
                        both = mine[j] * theirs
                        sums[j * len(pairs) + p] = sums[j * len(pairs) + p] + (both[:8] + both[8:])
            return tuple(sums)

        sums = lax.fori_loop(0, ny // TILE, body, sums, unroll=4)
    for j in (0, 1):
        for p, (k, s) in enumerate(pairs):
            out[j, (run ^ k) * count + s] = sums[j * len(pairs) + p]


def inner(first, second, fields, at):
    vmem = pl.BlockSpec(memory_space=pltpu.VMEM)
    operands = [in_vmem(a) for a in (first, *second, *fields)]
    return pl.pallas_call(
        functools.partial(inner_kernel, pieces=len(second), at=at),
        out_shape=jax.ShapeDtypeStruct((2, fields[0].shape[0] * len(fields), 8, 128), jnp.float32),
        in_specs=[vmem] * len(operands),
        out_specs=vmem,
        compiler_params=pltpu.CompilerParams(vmem_limit_bytes=2 * 1024 * 1024),
        cost_estimate=cost(2),
        name="inner",
    )(*operands)


def permute(array, axis, target):
    size = lax.axis_size(axis)
    return lax.ppermute(array, axis, [(i, target(i, size)) for i in range(size)])


def each(arrays, target):
    got = []
    for array in arrays:
        got.append(permute(array, "space", target))
    return tuple(got)


def swap(arrays):
    return each(arrays, lambda i, n: i ^ 1)


def shift(arrays):
    return each(arrays, lambda i, n: (i + 2 - 4 * (i % 2)) % n)


def gather(chunk, c, near, runs):
    got, at = [chunk, *near[1:]], [()] + [(c,)] * (len(near) - 1)
    half = runs // 2
    got.append(permute(chunk, "run", lambda i, n: i ^ half))
    bit = half // 2
    base = {half: got[-1]}
    while bit > 0:
        for k in list(base):
            base[k ^ bit] = permute(base[k], "run", lambda i, n: i ^ bit)
        bit //= 2
    return got[:half] + [base[k] for k in range(half, runs)], at + [()] * (runs - half)


def gather_near(snaps, runs):
    got = {0: snaps}
    bit = runs // 4
    while bit > 0:
        for k in list(got):
            got[k ^ bit] = permute(got[k], "run", lambda i, n: i ^ bit)
        bit //= 2
    return [got[k] for k in range(runs // 2)]


def on_device(adjoint_init, forward_snaps, base_speed, fwd_times, adj_times, horizon):
    runs, spaces = lax.axis_size("run"), lax.axis_size("space")
    _, parts, planes, ny, nz = adjoint_init.shape
    current = [(adjoint_init, (0, c)) for c in range(parts)]
    *halves, chunk = rounded(adjoint_init, forward_snaps, 0)
    rest, chunks, coefficients, around_z = prepare(adjoint_init, forward_snaps, base_speed)
    sent = [tuple(halves)] + [(field,) for field in rest]
    chunks = [chunk, *chunks]
    fields, sums = [], [None] * (SNAP // 2)
    swapped, shifted = {}, {}
    for c in range(parts):
        swapped[0, c] = swap(sent[c])
    near = gather_near(forward_snaps, runs)
    for c in range(parts):
        fields.append(gather(chunks[c], c, near, runs))
    for phase in range(SNAP // 2):
        kept = None
        for c in range(parts):
            if phase > 0:
                swapped[phase, c] = swap(sent[c])
            shifted[phase, c] = shift(swapped[phase, c])
            others = kept if c == 1 else None
            split = 2 if (phase, c) == (SNAP // 2 - 2, parts - 1) else 1
            halos = swapped[phase, c], shifted[phase, c]
            result = evolve(coefficients, around_z, *current[c], *halos, others, keep=(c == 0), split=split)
            current[c], first = (result[0], ()), result[1]
            sent[c] = tuple(result[2 : 2 + split])
            if c == 0:
                kept = result[2 + split :]
            part = inner(first, sent[c], *fields[c])
            sums[phase] = part if c == 0 else sums[phase] + part
    columns = jnp.stack(sums).reshape(SNAP, -1, 8, 128).sum((2, 3))
    bit = 1
    while bit < spaces:
        columns = columns + permute(columns, "space", lambda i, n: i ^ bit)
        bit *= 2
    summed = columns[None]
    scale = 1.0 / math.sqrt(parts * planes * spaces * ny * nz)
    inside = adj_times[:, :, None] + fwd_times[None, None, :] <= horizon[:, None, None]
    hankel = jnp.where(inside, summed * scale, jnp.zeros_like(summed))
    return (jnp.stack([q for q, _ in current])[None], hankel)


def solution(mesh):
    in_specs = (
        P("run", None, "space", None, None),
        P("run", None, "space", None, None),
        P(),
        P(),
        P("run", None),
        P("run"),
    )
    out_specs = (P("run", None, "space", None, None), P("run", None, None))
    return jax.shard_map(
        on_device, mesh=mesh, in_specs=in_specs, out_specs=out_specs, check_vma=False
    )
```

time: 132 us -> 131 us (level)
  waiting for transfers between devices: 37.8 us -> 72.2 us
  Pallas kernels: 47.5 us -> 29.3 us
  local copies, waits for them, and re-layouts: 16.3 us -> 0.69 us
    ppermute x22 -> x26, waiting for transfers between devices: 37.8 us -> 72.2 us  [permute(): lax.ppermute(array, axis, [(i, target(i, size)) for i in range(size)])]
    pallas_call x15 -> x14, Pallas kernels: 47.5 us -> 29.3 us  [the longest x6 18.7 us: evolve(): pl.pallas_call(functools.partial(evolve_kernel, coupled=coupled, planes=p...]
    unnamed x52 -> x8, local copies, waits for them, and re-layouts: 13.1 us -> 0.69 us
    squeeze x1 -> x0, local copies, waits for them, and re-layouts: 3.05 us -> none  [gather(): got.append(permute(snaps[:, c], 'run', lambda i, n: i ^ half))]
    ppermute x22 -> x26, starting transfers between devices: 24.9 us -> 24.4 us  [permute(): lax.ppermute(array, axis, [(i, target(i, size)) for i in range(size)])]
  transfers between devices with their start and end apart: 22 -> 26, of which waited for: 11 -> 15; matrix products, arithmetic and copies ran while one was open for 4% -> 1% of each run, Pallas kernels for 27% -> 17%
where the time goes in v1:
time: 131 us; the launch traced here: 130 us
  waiting for transfers between devices  72.2 us (55%)
  Pallas kernels  29.3 us (22%)
  starting transfers between devices  24.4 us (19%)
  other arithmetic  2.38 us (2%)
  between operations  1.5 us (1%)
    ppermute x26, waiting for transfers between devices, permute(): lax.ppermute(array, axis, [(i, target(i, size)) for i in range(size)])  72.2 us
    ppermute x26, starting transfers between devices, permute(): lax.ppermute(array, axis, [(i, target(i, size)) for i in range(size)])  24.4 us
    pallas_call x6, Pallas kernels, evolve(): pl.pallas_call(functools.partial(evolve_kernel, coupled=coupled, planes=p...  18.7 us
    pallas_call x6, Pallas kernels, inner(): pl.pallas_call(functools.partial(inner_kernel, pieces=len(second), at=at)...  6.84 us
  transfers between devices with their start and end apart: 26, of which 15 were waited for; matrix products, arithmetic and copies ran while one was open for 1% of the time, Pallas kernels for 17%

profile of v1, /device:TPU:0, one launch (start us, length us, event | category | flops | bytes accessed | tf_op | source)
XLA Modules:
  0.0 130.5 jit_solution(9782356024739496058)
XLA Ops:
  0.6 0.7 copy-done
  1.3 2.1 %prepare.1 = (bf16[4,192,256]{2,1,0:T(8,128)(2,1)S(1)}, bf16[4,192,256]{2,1,0:T(8,128)(2,1)S(1)}, bf16[2,4,192,256]{3,2,1,0:T(8,128)(2,1)S(1)}, bf16[2,4,192,256...) custom-call(f32[1,3,4,192,256]{4,3,2,1,0:T(8,128)} %refs_2_.5, ...), custom_call_target="tpu_custom_call" | custom-call | bytes 6000000 | tf_op jit(solution)/shard_map/prepare/pallas_call | solution.py:211
  3.4 3.1 %collective-permute-start.10 = (bf16[4,192,256]{2,1,0:T(8,128)(2,1)S(1)}, bf16[4,192,256]{2,1,0:T(8,128)(2,1)S(1)}, u32[]{:S(2)}, u32[]{:S(2)}) collective-permute-start(bf16[4,192,256]{2,1,0:T(8,128)(2,1)S(1)} %get-tuple-element.57), channel_id=1, source_target_pairs={{0,1},{1,0},{2,3},{3,2},{4,5},{5,4},{6,7},{7,6},{8,9},{9,8},{10,11... | collective-permute-start | bytes 1179656 | tf_op jit(solution)/shard_map/ppermute | solution.py:277
  6.5 1.7 %rounded.1 = (bf16[2,192,256]{2,1,0:T(8,128)(2,1)S(1)}, bf16[2,192,256]{2,1,0:T(8,128)(2,1)S(1)}, bf16[2,4,192,256]{3,2,1,0:T(8,128)(2,1)S(1)}) custom-call(f32[1,3,4,192,256]{4,3,2,1,0:T(8,128)} %refs_2_.5, bf16[2,3,4,192,256]{4,3,2,1,0:T(8,128)(2,1)} %snaps.3), custom_call_target="tpu_custom_call" | custom-call | bytes 3000000 | tf_op jit(solution)/shard_map/rounded/pallas_call | solution.py:149
  8.2 1.9 %collective-permute-start = (bf16[2,192,256]{2,1,0:T(8,128)(2,1)S(1)}, bf16[2,192,256]{2,1,0:T(8,128)(2,1)S(1)}, u32[]{:S(2)}, u32[]{:S(2)}) collective-permute-start(bf16[2,192,256]{2,1,0:T(8,128)(2,1)S(1)} %get-tuple-element.40), channel_id=1, source_target_pairs={{0,1},{1,0},{2,3},{3,2},{4,5},{5,4},{6,7},{7,6},{8,9},{9,8},{10,11... | collective-permute-start | bytes 589832 | tf_op jit(solution)/shard_map/ppermute | solution.py:277
  10.1 0.2 collective-permute-start.1
  10.3 18.8 %collective-permute-done.refs_3_ = bf16[2,192,256]{2,1,0:T(8,128)(2,1)S(1)} collective-permute-done((bf16[2,192,256]{2,1,0:T(8,128)(2,1)S(1)}, bf16[2,192,256]{2,1,0:T(8,128)(2,1)S(1)}, u32[]{:S(2)}, u32[]{:S(2)}) %collective-permute-start) | collective-permute-done | bytes 196640 | tf_op jit(solution)/shard_map/ppermute | solution.py:277
  29.0 2.1 %collective-permute-start.2 = (bf16[2,192,256]{2,1,0:T(8,128)(2,1)S(1)}, bf16[2,192,256]{2,1,0:T(8,128)(2,1)S(1)}, u32[]{:S(2)}, u32[]{:S(2)}) collective-permute-start(bf16[2,192,256]{2,1,0:T(8,128)(2,1)S(1)} %collective-permute-done.refs_3_), channel_id=1, source_target_pairs={{0,2},{1,7},{2,4},{3,1},{4,6},{5,3},{6,0},{7,5},{8,10},{9,15},{10,... | collective-permute-start | bytes 589832 | tf_op jit(solution)/shard_map/ppermute | solution.py:277
  31.1 1.3 collective-permute-done.1.refs_4_
  32.4 1.8 %collective-permute-start.3 = (bf16[2,192,256]{2,1,0:T(8,128)(2,1)S(1)}, bf16[2,192,256]{2,1,0:T(8,128)(2,1)S(1)}, u32[]{:S(2)}, u32[]{:S(2)}) collective-permute-start(bf16[2,192,256]{2,1,0:T(8,128)(2,1)S(1)} %collective-permute-done.1.refs_4_), channel_id=1, source_target_pairs={{0,2},{1,7},{2,4},{3,1},{4,6},{5,3},{6,0},{7,5},{8,10},{9,15},{10,... | collective-permute-start | bytes 589832 | tf_op jit(solution)/shard_map/ppermute | solution.py:277
  34.2 1.6 %collective-permute-start.11 = (bf16[4,192,256]{2,1,0:T(8,128)(2,1)S(1)}, bf16[4,192,256]{2,1,0:T(8,128)(2,1)S(1)}, u32[]{:S(2)}, u32[]{:S(2)}) collective-permute-start(bf16[4,192,256]{2,1,0:T(8,128)(2,1)S(1)} %collective-permute-done.10.refs_3_), channel_id=1, source_target_pairs={{0,2},{1,7},{2,4},{3,1},{4,6},{5,3},{6,0},{7,5},{8,10},{9,15},{10,... | collective-permute-start | bytes 1179656 | tf_op jit(solution)/shard_map/ppermute | solution.py:277
  35.8 1.6 %collective-permute-start.7 = (bf16[4,192,256]{2,1,0:T(8,128)(2,1)S(1)}, bf16[4,192,256]{2,1,0:T(8,128)(2,1)S(1)}, u32[]{:S(2)}, u32[]{:S(2)}) collective-permute-start(bf16[4,192,256]{2,1,0:T(8,128)(2,1)S(1)} %collective-permute-done.6.refs_3_), channel_id=1, source_target_pairs={{0,2},{1,7},{2,4},{3,1},{4,6},{5,3},{6,0},{7,5},{8,10},{9,15},{10,... | collective-permute-start | bytes 1179656 | tf_op jit(solution)/shard_map/ppermute | solution.py:277
  37.5 1.9 %collective-permute-start.21 = (bf16[2,4,192,256]{3,2,1,0:T(8,128)(2,1)S(1)}, bf16[2,4,192,256]{3,2,1,0:T(8,128)(2,1)S(1)}, u32[]{:S(2)}, u32[]{:S(2)}) collective-permute-start(bf16[2,4,192,256]{3,2,1,0:T(8,128)(2,1)S(1)} %get-tuple-element.67.refs_3_.refs_2_), channel_id=1, source_target_pairs={{0,16},{8,24},{16,0},{24,8},{1,17},{9,25},{17,1},{25,9},{2,18},{10... | collective-permute-start | bytes 2359304 | tf_op jit(solution)/shard_map/ppermute | solution.py:277
  39.4 2.5 %collective-permute-done.3.refs_6_ = bf16[2,192,256]{2,1,0:T(8,128)(2,1)S(1)} collective-permute-done((bf16[2,192,256]{2,1,0:T(8,128)(2,1)S(1)}, bf16[2,192,256]{2,1,0:T(8,128)(2,1)S(1)}, u32[]{:S(2)}, u32[]{:S(2)}) %collective-permute-start.3) | collective-permute-done | bytes 196640 | tf_op jit(solution)/shard_map/ppermute | solution.py:277
  42.0 1.7 %collective-permute-start.17 = (bf16[2,4,192,256]{3,2,1,0:T(8,128)(2,1)S(1)}, bf16[2,4,192,256]{3,2,1,0:T(8,128)(2,1)S(1)}, u32[]{:S(2)}, u32[]{:S(2)}) collective-permute-start(bf16[2,4,192,256]{3,2,1,0:T(8,128)(2,1)S(1)} %get-tuple-element.63.refs_2_), channel_id=1, source_target_pairs={{0,16},{8,24},{16,0},{24,8},{1,17},{9,25},{17,1},{25,9},{2,18},{10... | collective-permute-start | bytes 2359304 | tf_op jit(solution)/shard_map/ppermute | solution.py:277
  43.7 6.7 %collective-permute-done.11.refs_4_ = bf16[4,192,256]{2,1,0:T(8,128)(2,1)S(1)} collective-permute-done((bf16[4,192,256]{2,1,0:T(8,128)(2,1)S(1)}, bf16[4,192,256]{2,1,0:T(8,128)(2,1)S(1)}, u32[]{:S(2)}, u32[]{:S(2)}) %collective-permute-start.11) | collective-permute-done | bytes 393248 | tf_op jit(solution)/shard_map/ppermute | solution.py:277
  50.4 1.7 %collective-permute-start.19 = (bf16[2,4,192,256]{3,2,1,0:T(8,128)(2,1)S(1)}, bf16[2,4,192,256]{3,2,1,0:T(8,128)(2,1)S(1)}, u32[]{:S(2)}, u32[]{:S(2)}) collective-permute-start(bf16[2,4,192,256]{3,2,1,0:T(8,128)(2,1)S(1)} %get-tuple-element.65.refs_2_), channel_id=1, source_target_pairs={{0,16},{8,24},{16,0},{24,8},{1,17},{9,25},{17,1},{25,9},{2,18},{10... | collective-permute-start | bytes 2359304 | tf_op jit(solution)/shard_map/ppermute | solution.py:277
  52.1 3.6 %evolve_u.2 = (f32[4,192,256]{2,1,0:T(8,128)S(1)}, bf16[4,192,256]{2,1,0:T(8,128)(2,1)S(1)}, bf16[4,192,256]{2,1,0:T(8,128)(2,1)S(1)}, f32[12,2,208,128]{3,2,1,0...) custom-call(f32[6,192,128]{2,1,0:T(8,128)S(1)} %get-tuple-element.38., ...), custom_call_target="tpu_custom_call" | custom-call | bytes 13500000 | tf_op jit(solution)/shard_map/evolve_u/pallas_call | solution.py:116
  55.7 2.1 %collective-permute-done.7.refs_4_ = bf16[4,192,256]{2,1,0:T(8,128)(2,1)S(1)} collective-permute-done((bf16[4,192,256]{2,1,0:T(8,128)(2,1)S(1)}, bf16[4,192,256]{2,1,0:T(8,128)(2,1)S(1)}, u32[]{:S(2)}, u32[]{:S(2)}) %collective-permute-start.7) | collective-permute-done | bytes 393248 | tf_op jit(solution)/shard_map/ppermute | solution.py:277
  57.9 1.1 collective-permute-start.4
  58.9 3.5 %evolve_w.2 = (f32[4,192,256]{2,1,0:T(8,128)S(1)}, bf16[4,192,256]{2,1,0:T(8,128)(2,1)S(1)}, bf16[2,192,256]{2,1,0:T(8,128)(2,1)S(1)}, bf16[2,192,256]{2,1,0:T(8,128)(2,1)S(1)}) custom-call(f32[6,192,128]{2,1,0:T(8,128)S(1)} %get-tuple-element.38.refs_0_, bf16[256,256]{1,0:T(8,128)(2,1)S(1)} %get-tuple-element.39.refs_1_, f32[1,3,4,192,256]{4,3,2,1,0:T(8,128)} %refs_2_.5, ...), custom_call_target="tpu_custom_call" | custom-call | bytes 13500000 | tf_op jit(solution)/shard_map/evolve_w/pallas_call | solution.py:116
  62.4 5.6 %collective-permute-done.4.refs_3_ = bf16[4,192,256]{2,1,0:T(8,128)(2,1)S(1)} collective-permute-done((bf16[4,192,256]{2,1,0:T(8,128)(2,1)S(1)}, bf16[4,192,256]{2,1,0:T(8,128)(2,1)S(1)}, u32[]{:S(2)}, u32[]{:S(2)}) %collective-permute-start.4) | collective-permute-done | bytes 393248 | tf_op jit(solution)/shard_map/ppermute | solution.py:277
  68.0 1.0 collective-permute-start.12
  69.0 1.0 collective-permute-start.13
  70.0 3.8 %evolve_v.2 = (f32[4,192,256]{2,1,0:T(8,128)S(1)}, bf16[4,192,256]{2,1,0:T(8,128)(2,1)S(1)}, bf16[4,192,256]{2,1,0:T(8,128)(2,1)S(1)}) custom-call(f32[6,192,128]{2,1,0:T(8,128)S(1)} %get-tuple-element.38.refs_0_, bf16[256,256]{1,0:T(8,128)(2,1)S(1)} %get-tuple-element.39.refs_1_, f32[1,3,4,192,256]{4,3,2,1,0:T(8,128)} %refs_2_.5, ...), custom_call_target="tpu_custom_call" | custom-call | bytes 13500000 | tf_op jit(solution)/shard_map/evolve_v/pallas_call | solution.py:116
  73.8 0.9 collective-permute-done.17.refs_4_
  74.8 1.3 %collective-permute-start.8 = (bf16[4,192,256]{2,1,0:T(8,128)(2,1)S(1)}, bf16[4,192,256]{2,1,0:T(8,128)(2,1)S(1)}, u32[]{:S(2)}, u32[]{:S(2)}) collective-permute-start(bf16[4,192,256]{2,1,0:T(8,128)(2,1)S(1)} %get-tuple-element.51.refs_1_), channel_id=1, source_target_pairs={{0,1},{1,0},{2,3},{3,2},{4,5},{5,4},{6,7},{7,6},{8,9},{9,8},{10,11... | collective-permute-start | bytes 1179656 | tf_op jit(solution)/shard_map/ppermute | solution.py:277
  76.1 1.4 %collective-permute-start.14 = (bf16[2,192,256]{2,1,0:T(8,128)(2,1)S(1)}, bf16[2,192,256]{2,1,0:T(8,128)(2,1)S(1)}, u32[]{:S(2)}, u32[]{:S(2)}) collective-permute-start(bf16[2,192,256]{2,1,0:T(8,128)(2,1)S(1)} %collective-permute-done.12.refs_3_), channel_id=1, source_target_pairs={{0,2},{1,7},{2,4},{3,1},{4,6},{5,3},{6,0},{7,5},{8,10},{9,15},{10,... | collective-permute-start | bytes 589832 | tf_op jit(solution)/shard_map/ppermute | solution.py:277
  77.5 2.5 %collective-permute-done.13.refs_4_ = bf16[2,192,256]{2,1,0:T(8,128)(2,1)S(1)} collective-permute-done((bf16[2,192,256]{2,1,0:T(8,128)(2,1)S(1)}, bf16[2,192,256]{2,1,0:T(8,128)(2,1)S(1)}, u32[]{:S(2)}, u32[]{:S(2)}) %collective-permute-start.13) | collective-permute-done | bytes 196640 | tf_op jit(solution)/shard_map/ppermute | solution.py:277
  80.0 8.7 %collective-permute-done.19.refs_4_ = bf16[2,4,192,256]{3,2,1,0:T(8,128)(2,1)S(1)} collective-permute-done((bf16[2,4,192,256]{3,2,1,0:T(8,128)(2,1)S(1)}, bf16[2,4,192,256]{3,2,1,0:T(8,128)(2,1)S(1)}, u32[]{:S(2)}, u32[]{:S(2)}) %collective-permute-start.19) | collective-permute-done | bytes 786464 | tf_op jit(solution)/shard_map/ppermute | solution.py:277
  88.7 0.3 collective-permute-start.5
  89.0 0.5 collective-permute-start.18
  89.6 9.0 %collective-permute-done.5.refs_4_ = bf16[4,192,256]{2,1,0:T(8,128)(2,1)S(1)} collective-permute-done((bf16[4,192,256]{2,1,0:T(8,128)(2,1)S(1)}, bf16[4,192,256]{2,1,0:T(8,128)(2,1)S(1)}, u32[]{:S(2)}, u32[]{:S(2)}) %collective-permute-start.5) | collective-permute-done | bytes 393248 | tf_op jit(solution)/shard_map/ppermute | solution.py:277
  98.6 2.6 %evolve_u.3 = (f32[4,192,256]{2,1,0:T(8,128)S(1)}, bf16[4,192,256]{2,1,0:T(8,128)(2,1)S(1)}, bf16[4,192,256]{2,1,0:T(8,128)(2,1)S(1)}, f32[12,2,208,128]{3,2,1,0...) custom-call(f32[6,192,128]{2,1,0:T(8,128)S(1)} %get-tuple-element.38., ...), custom_call_target="tpu_custom_call" | custom-call | bytes 13500000 | tf_op jit(solution)/shard_map/evolve_u/pallas_call | solution.py:116
  101.2 2.5 %evolve_w.3 = (f32[4,192,256]{2,1,0:T(8,128)S(1)}, bf16[4,192,256]{2,1,0:T(8,128)(2,1)S(1)}, bf16[4,192,256]{2,1,0:T(8,128)(2,1)S(1)}) custom-call(f32[6,192,128]{2,1,0:T(8,128)S(1)} %get-tuple-element.38.refs_0_, bf16[256,256]{1,0:T(8,128)(2,1)S(1)} %get-tuple-element.39.refs_1_, f32[4,192,256]{2,1,0:T(8,128)S(1)} %get-tuple-element.58.refs_2_, ...), custom_call_target="tpu_custom_call" | custom-call | bytes 13500000 | tf_op jit(solution)/shard_map/evolve_w/pallas_call | solution.py:116
  103.7 4.5 %collective-permute-done.9.refs_4_ = bf16[4,192,256]{2,1,0:T(8,128)(2,1)S(1)} collective-permute-done((bf16[4,192,256]{2,1,0:T(8,128)(2,1)S(1)}, bf16[4,192,256]{2,1,0:T(8,128)(2,1)S(1)}, u32[]{:S(2)}, u32[]{:S(2)}) %collective-permute-start.9) | collective-permute-done | bytes 393248 | tf_op jit(solution)/shard_map/ppermute | solution.py:277
  108.2 2.8 %evolve_v.3 = (f32[4,192,256]{2,1,0:T(8,128)S(1)}, bf16[4,192,256]{2,1,0:T(8,128)(2,1)S(1)}, bf16[4,192,256]{2,1,0:T(8,128)(2,1)S(1)}) custom-call(f32[6,192,128]{2,1,0:T(8,128)S(1)} %get-tuple-element.38.refs_0_, bf16[256,256]{1,0:T(8,128)(2,1)S(1)} %get-tuple-element.39.refs_1_, f32[4,192,256]{2,1,0:T(8,128)S(1)} %get-tuple-element.50.refs_2_, ...), custom_call_target="tpu_custom_call" | custom-call | bytes 13500000 | tf_op jit(solution)/shard_map/evolve_v/pallas_call | solution.py:116
  111.0 1.1 inner.11
  112.2 1.1 inner.9
  113.3 1.1 inner.10
  114.5 1.1 inner.8
  115.6 1.1 inner.6
  116.8 1.1 inner.7
  118.2 3.6 %collective-permute-done.23 = f32[4,8]{1,0:T(4,128)S(1)} collective-permute-done((f32[4,8]{1,0:T(4,128)S(1)}, f32[4,8]{1,0:T(4,128)S(1)}, u32[]{:S(2)}, u32[]{:S(2)}) %collective-permute-start.23) | collective-permute-done | bytes 160 | tf_op jit(solution)/shard_map/ppermute | solution.py:277
  122.4 2.9 %collective-permute-done.24 = f32[4,8]{1,0:T(4,128)S(1)} collective-permute-done((f32[4,8]{1,0:T(4,128)S(1)}, f32[4,8]{1,0:T(4,128)S(1)}, u32[]{:S(2)}, u32[]{:S(2)}) %collective-permute-start.24) | collective-permute-done | bytes 160 | tf_op jit(solution)/shard_map/ppermute | solution.py:277
  125.4 1.6 %maximum_bitcast_fusion = f32[1,3,4,192,256]{4,3,2,1,0:T(8,128)} fusion(f32[1,4,192,256]{3,2,1,0:T(8,128)S(1)} %bitcast.17, f32[1,4,192,256]{3,2,1,0:T(8,128)S(1)} %bitcast.18, f32[1,4,192,256]{3,2,1,0:T(8,128)S(1)} %bitcast.16), kind=kLoop, calls=%fused_computation | loop fusion | flops 1179648 | bytes 4718592 | tf_op jit(solution)/shard_map/broadcast_in_dim | solution.py:358
  126.9 2.9 %collective-permute-done.25 = f32[4,8]{1,0:T(4,128)S(1)} collective-permute-done((f32[4,8]{1,0:T(4,128)S(1)}, f32[4,8]{1,0:T(4,128)S(1)}, u32[]{:S(2)}, u32[]{:S(2)}) %collective-permute-start.25) | collective-permute-done | bytes 160 | tf_op jit(solution)/shard_map/ppermute | solution.py:277
  129.8 0.6 select_bitcast_fusion
  (33 shorter events, 0.6 us)
Async XLA Ops:
  0.6 0.7 copy-start
  3.4 30.8 %collective-permute-start.10 = (bf16[4,192,256]{2,1,0:T(8,128)(2,1)S(1)}, bf16[4,192,256]{2,1,0:T(8,128)(2,1)S(1)}, u32[]{:S(2)}, u32[]{:S(2)}) collective-permute-start(bf16[4,192,256]{2,1,0:T(8,128)(2,1)S(1)} %get-tuple-element.57), channel_id=1, source_target_pairs={{0,1},{1,0},{2,3},{3,2},{4,5},{5,4},{6,7},{7,6},{8,9},{9,8},{10,11... | collective-permute-start | bytes 1179656 | tf_op jit(solution)/shard_map/ppermute | solution.py:277
  6.4 3.6 %copy-start.1 = (bf16[2,3,4,192,256]{4,3,2,1,0:T(8,128)(2,1)S(1)}, bf16[2,3,4,192,256]{4,3,2,1,0:T(8,128)(2,1)}, u32[]{:S(2)}) copy-start(bf16[2,3,4,192,256]{4,3,2,1,0:T(8,128)(2,1)} %snaps.3) | copy-start | bytes 7077892
  6.4 29.3 %collective-permute-start.6 = (bf16[4,192,256]{2,1,0:T(8,128)(2,1)S(1)}, bf16[4,192,256]{2,1,0:T(8,128)(2,1)S(1)}, u32[]{:S(2)}, u32[]{:S(2)}) collective-permute-start(bf16[4,192,256]{2,1,0:T(8,128)(2,1)S(1)} %get-tuple-element.45), channel_id=1, source_target_pairs={{0,1},{1,0},{2,3},{3,2},{4,5},{5,4},{6,7},{7,6},{8,9},{9,8},{10,11... | collective-permute-start | bytes 1179656 | tf_op jit(solution)/shard_map/ppermute | solution.py:277
  8.2 20.9 %collective-permute-start = (bf16[2,192,256]{2,1,0:T(8,128)(2,1)S(1)}, bf16[2,192,256]{2,1,0:T(8,128)(2,1)S(1)}, u32[]{:S(2)}, u32[]{:S(2)}) collective-permute-start(bf16[2,192,256]{2,1,0:T(8,128)(2,1)S(1)} %get-tuple-element.40), channel_id=1, source_target_pairs={{0,1},{1,0},{2,3},{3,2},{4,5},{5,4},{6,7},{7,6},{8,9},{9,8},{10,11... | collective-permute-start | bytes 589832 | tf_op jit(solution)/shard_map/ppermute | solution.py:277
  10.1 100.9 %collective-permute-start.16 = (bf16[2,3,4,192,256]{4,3,2,1,0:T(8,128)(2,1)S(1)}, bf16[2,3,4,192,256]{4,3,2,1,0:T(8,128)(2,1)S(1)}, u32[]{:S(2)}, u32[]{:S(2)}) collective-permute-start(bf16[2,3,4,192,256]{4,3,2,1,0:T(8,128)(2,1)S(1)} %copy-done.1), channel_id=1, source_target_pairs={{0,8},{8,0},{16,24},{24,16},{1,9},{9,1},{17,25},{25,17},{2,10},{10... | collective-permute-start | bytes 7077896 | tf_op jit(solution)/shard_map/ppermute | solution.py:277
  10.1 22.3 %collective-permute-start.1 = (bf16[2,192,256]{2,1,0:T(8,128)(2,1)S(1)}, bf16[2,192,256]{2,1,0:T(8,128)(2,1)S(1)}, u32[]{:S(2)}, u32[]{:S(2)}) collective-permute-start(bf16[2,192,256]{2,1,0:T(8,128)(2,1)S(1)} %get-tuple-element.41), channel_id=1, source_target_pairs={{0,1},{1,0},{2,3},{3,2},{4,5},{5,4},{6,7},{7,6},{8,9},{9,8},{10,11... | collective-permute-start | bytes 589832 | tf_op jit(solution)/shard_map/ppermute | solution.py:277
  29.0 8.5 %collective-permute-start.2 = (bf16[2,192,256]{2,1,0:T(8,128)(2,1)S(1)}, bf16[2,192,256]{2,1,0:T(8,128)(2,1)S(1)}, u32[]{:S(2)}, u32[]{:S(2)}) collective-permute-start(bf16[2,192,256]{2,1,0:T(8,128)(2,1)S(1)} %collective-permute-done.refs_3_), channel_id=1, source_target_pairs={{0,2},{1,7},{2,4},{3,1},{4,6},{5,3},{6,0},{7,5},{8,10},{9,15},{10,... | collective-permute-start | bytes 589832 | tf_op jit(solution)/shard_map/ppermute | solution.py:277
  32.4 9.6 %collective-permute-start.3 = (bf16[2,192,256]{2,1,0:T(8,128)(2,1)S(1)}, bf16[2,192,256]{2,1,0:T(8,128)(2,1)S(1)}, u32[]{:S(2)}, u32[]{:S(2)}) collective-permute-start(bf16[2,192,256]{2,1,0:T(8,128)(2,1)S(1)} %collective-permute-done.1.refs_4_), channel_id=1, source_target_pairs={{0,2},{1,7},{2,4},{3,1},{4,6},{5,3},{6,0},{7,5},{8,10},{9,15},{10,... | collective-permute-start | bytes 589832 | tf_op jit(solution)/shard_map/ppermute | solution.py:277
  34.2 16.2 %collective-permute-start.11 = (bf16[4,192,256]{2,1,0:T(8,128)(2,1)S(1)}, bf16[4,192,256]{2,1,0:T(8,128)(2,1)S(1)}, u32[]{:S(2)}, u32[]{:S(2)}) collective-permute-start(bf16[4,192,256]{2,1,0:T(8,128)(2,1)S(1)} %collective-permute-done.10.refs_3_), channel_id=1, source_target_pairs={{0,2},{1,7},{2,4},{3,1},{4,6},{5,3},{6,0},{7,5},{8,10},{9,15},{10,... | collective-permute-start | bytes 1179656 | tf_op jit(solution)/shard_map/ppermute | solution.py:277
  35.8 22.1 %collective-permute-start.7 = (bf16[4,192,256]{2,1,0:T(8,128)(2,1)S(1)}, bf16[4,192,256]{2,1,0:T(8,128)(2,1)S(1)}, u32[]{:S(2)}, u32[]{:S(2)}) collective-permute-start(bf16[4,192,256]{2,1,0:T(8,128)(2,1)S(1)} %collective-permute-done.6.refs_3_), channel_id=1, source_target_pairs={{0,2},{1,7},{2,4},{3,1},{4,6},{5,3},{6,0},{7,5},{8,10},{9,15},{10,... | collective-permute-start | bytes 1179656 | tf_op jit(solution)/shard_map/ppermute | solution.py:277
  37.5 31.5 %collective-permute-start.21 = (bf16[2,4,192,256]{3,2,1,0:T(8,128)(2,1)S(1)}, bf16[2,4,192,256]{3,2,1,0:T(8,128)(2,1)S(1)}, u32[]{:S(2)}, u32[]{:S(2)}) collective-permute-start(bf16[2,4,192,256]{3,2,1,0:T(8,128)(2,1)S(1)} %get-tuple-element.67.refs_3_.refs_2_), channel_id=1, source_target_pairs={{0,16},{8,24},{16,0},{24,8},{1,17},{9,25},{17,1},{25,9},{2,18},{10... | collective-permute-start | bytes 2359304 | tf_op jit(solution)/shard_map/ppermute | solution.py:277
  42.0 32.8 %collective-permute-start.17 = (bf16[2,4,192,256]{3,2,1,0:T(8,128)(2,1)S(1)}, bf16[2,4,192,256]{3,2,1,0:T(8,128)(2,1)S(1)}, u32[]{:S(2)}, u32[]{:S(2)}) collective-permute-start(bf16[2,4,192,256]{3,2,1,0:T(8,128)(2,1)S(1)} %get-tuple-element.63.refs_2_), channel_id=1, source_target_pairs={{0,16},{8,24},{16,0},{24,8},{1,17},{9,25},{17,1},{25,9},{2,18},{10... | collective-permute-start | bytes 2359304 | tf_op jit(solution)/shard_map/ppermute | solution.py:277
  50.4 38.3 %collective-permute-start.19 = (bf16[2,4,192,256]{3,2,1,0:T(8,128)(2,1)S(1)}, bf16[2,4,192,256]{3,2,1,0:T(8,128)(2,1)S(1)}, u32[]{:S(2)}, u32[]{:S(2)}) collective-permute-start(bf16[2,4,192,256]{3,2,1,0:T(8,128)(2,1)S(1)} %get-tuple-element.65.refs_2_), channel_id=1, source_target_pairs={{0,16},{8,24},{16,0},{24,8},{1,17},{9,25},{17,1},{25,9},{2,18},{10... | collective-permute-start | bytes 2359304 | tf_op jit(solution)/shard_map/ppermute | solution.py:277
  57.9 10.2 %collective-permute-start.4 = (bf16[4,192,256]{2,1,0:T(8,128)(2,1)S(1)}, bf16[4,192,256]{2,1,0:T(8,128)(2,1)S(1)}, u32[]{:S(2)}, u32[]{:S(2)}) collective-permute-start(bf16[4,192,256]{2,1,0:T(8,128)(2,1)S(1)} %get-tuple-element.43.refs_1_), channel_id=1, source_target_pairs={{0,1},{1,0},{2,3},{3,2},{4,5},{5,4},{6,7},{7,6},{8,9},{9,8},{10,11... | collective-permute-start | bytes 1179656 | tf_op jit(solution)/shard_map/ppermute | solution.py:277
  68.0 8.1 %collective-permute-start.12 = (bf16[2,192,256]{2,1,0:T(8,128)(2,1)S(1)}, bf16[2,192,256]{2,1,0:T(8,128)(2,1)S(1)}, u32[]{:S(2)}, u32[]{:S(2)}) collective-permute-start(bf16[2,192,256]{2,1,0:T(8,128)(2,1)S(1)} %get-tuple-element.59.refs_1_), channel_id=1, source_target_pairs={{0,1},{1,0},{2,3},{3,2},{4,5},{5,4},{6,7},{7,6},{8,9},{9,8},{10,11... | collective-permute-start | bytes 589832 | tf_op jit(solution)/shard_map/ppermute | solution.py:277
  69.0 11.0 %collective-permute-start.13 = (bf16[2,192,256]{2,1,0:T(8,128)(2,1)S(1)}, bf16[2,192,256]{2,1,0:T(8,128)(2,1)S(1)}, u32[]{:S(2)}, u32[]{:S(2)}) collective-permute-start(bf16[2,192,256]{2,1,0:T(8,128)(2,1)S(1)} %get-tuple-element.60.refs_2_), channel_id=1, source_target_pairs={{0,1},{1,0},{2,3},{3,2},{4,5},{5,4},{6,7},{7,6},{8,9},{9,8},{10,11... | collective-permute-start | bytes 589832 | tf_op jit(solution)/shard_map/ppermute | solution.py:277
  74.8 14.7 %collective-permute-start.8 = (bf16[4,192,256]{2,1,0:T(8,128)(2,1)S(1)}, bf16[4,192,256]{2,1,0:T(8,128)(2,1)S(1)}, u32[]{:S(2)}, u32[]{:S(2)}) collective-permute-start(bf16[4,192,256]{2,1,0:T(8,128)(2,1)S(1)} %get-tuple-element.51.refs_1_), channel_id=1, source_target_pairs={{0,1},{1,0},{2,3},{3,2},{4,5},{5,4},{6,7},{7,6},{8,9},{9,8},{10,11... | collective-permute-start | bytes 1179656 | tf_op jit(solution)/shard_map/ppermute | solution.py:277
  76.1 12.9 %collective-permute-start.14 = (bf16[2,192,256]{2,1,0:T(8,128)(2,1)S(1)}, bf16[2,192,256]{2,1,0:T(8,128)(2,1)S(1)}, u32[]{:S(2)}, u32[]{:S(2)}) collective-permute-start(bf16[2,192,256]{2,1,0:T(8,128)(2,1)S(1)} %collective-permute-done.12.refs_3_), channel_id=1, source_target_pairs={{0,2},{1,7},{2,4},{3,1},{4,6},{5,3},{6,0},{7,5},{8,10},{9,15},{10,... | collective-permute-start | bytes 589832 | tf_op jit(solution)/shard_map/ppermute | solution.py:277
  80.0 9.0 %collective-permute-start.15 = (bf16[2,192,256]{2,1,0:T(8,128)(2,1)S(1)}, bf16[2,192,256]{2,1,0:T(8,128)(2,1)S(1)}, u32[]{:S(2)}, u32[]{:S(2)}) collective-permute-start(bf16[2,192,256]{2,1,0:T(8,128)(2,1)S(1)} %collective-permute-done.13.refs_4_), channel_id=1, source_target_pairs={{0,2},{1,7},{2,4},{3,1},{4,6},{5,3},{6,0},{7,5},{8,10},{9,15},{10,... | collective-permute-start | bytes 589832 | tf_op jit(solution)/shard_map/ppermute | solution.py:277
  88.7 9.9 %collective-permute-start.5 = (bf16[4,192,256]{2,1,0:T(8,128)(2,1)S(1)}, bf16[4,192,256]{2,1,0:T(8,128)(2,1)S(1)}, u32[]{:S(2)}, u32[]{:S(2)}) collective-permute-start(bf16[4,192,256]{2,1,0:T(8,128)(2,1)S(1)} %collective-permute-done.4.refs_3_), channel_id=1, source_target_pairs={{0,2},{1,7},{2,4},{3,1},{4,6},{5,3},{6,0},{7,5},{8,10},{9,15},{10,... | collective-permute-start | bytes 1179656 | tf_op jit(solution)/shard_map/ppermute | solution.py:277
  89.0 22.0 %collective-permute-start.22 = (bf16[2,4,192,256]{3,2,1,0:T(8,128)(2,1)S(1)}, bf16[2,4,192,256]{3,2,1,0:T(8,128)(2,1)S(1)}, u32[]{:S(2)}, u32[]{:S(2)}) collective-permute-start(bf16[2,4,192,256]{3,2,1,0:T(8,128)(2,1)S(1)} %collective-permute-done.21.refs_5_.refs_4_), channel_id=1, source_target_pairs={{0,8},{8,0},{16,24},{24,16},{1,9},{9,1},{17,25},{25,17},{2,10},{10... | collective-permute-start | bytes 2359304 | tf_op jit(solution)/shard_map/ppermute | solution.py:277
  89.0 23.1 %collective-permute-start.18 = (bf16[2,4,192,256]{3,2,1,0:T(8,128)(2,1)S(1)}, bf16[2,4,192,256]{3,2,1,0:T(8,128)(2,1)S(1)}, u32[]{:S(2)}, u32[]{:S(2)}) collective-permute-start(bf16[2,4,192,256]{3,2,1,0:T(8,128)(2,1)S(1)} %collective-permute-done.17.refs_4_), channel_id=1, source_target_pairs={{0,8},{8,0},{16,24},{24,16},{1,9},{9,1},{17,25},{25,17},{2,10},{10... | collective-permute-start | bytes 2359304 | tf_op jit(solution)/shard_map/ppermute | solution.py:277
  89.5 23.8 %collective-permute-start.20 = (bf16[2,4,192,256]{3,2,1,0:T(8,128)(2,1)S(1)}, bf16[2,4,192,256]{3,2,1,0:T(8,128)(2,1)S(1)}, u32[]{:S(2)}, u32[]{:S(2)}) collective-permute-start(bf16[2,4,192,256]{3,2,1,0:T(8,128)(2,1)S(1)} %collective-permute-done.19.refs_4_), channel_id=1, source_target_pairs={{0,8},{8,0},{16,24},{24,16},{1,9},{9,1},{17,25},{25,17},{2,10},{10... | collective-permute-start | bytes 2359304 | tf_op jit(solution)/shard_map/ppermute | solution.py:277
  98.6 9.6 %collective-permute-start.9 = (bf16[4,192,256]{2,1,0:T(8,128)(2,1)S(1)}, bf16[4,192,256]{2,1,0:T(8,128)(2,1)S(1)}, u32[]{:S(2)}, u32[]{:S(2)}) collective-permute-start(bf16[4,192,256]{2,1,0:T(8,128)(2,1)S(1)} %collective-permute-done.8.refs_3_), channel_id=1, source_target_pairs={{0,2},{1,7},{2,4},{3,1},{4,6},{5,3},{6,0},{7,5},{8,10},{9,15},{10,... | collective-permute-start | bytes 1179656 | tf_op jit(solution)/shard_map/ppermute | solution.py:277
  118.1 3.7 %collective-permute-start.23 = (f32[4,8]{1,0:T(4,128)S(1)}, f32[4,8]{1,0:T(4,128)S(1)}, u32[]{:S(2)}, u32[]{:S(2)}) collective-permute-start(f32[4,8]{1,0:T(4,128)S(1)} %bitcast.20), channel_id=1, source_target_pairs={{0,1},{1,0},{2,3},{3,2},{4,5},{5,4},{6,7},{7,6},{8,9},{9,8},{10,11... | collective-permute-start | bytes 392 | tf_op jit(solution)/shard_map/ppermute | solution.py:277
  121.8 3.6 %collective-permute-start.24 = (f32[4,8]{1,0:T(4,128)S(1)}, f32[4,8]{1,0:T(4,128)S(1)}, u32[]{:S(2)}, u32[]{:S(2)}) collective-permute-start(f32[4,8]{1,0:T(4,128)S(1)} %add.45), channel_id=1, source_target_pairs={{0,2},{1,3},{2,0},{3,1},{4,6},{5,7},{6,4},{7,5},{8,10},{9,11},{10,... | collective-permute-start | bytes 392 | tf_op jit(solution)/shard_map/ppermute | solution.py:277
  125.4 4.5 %collective-permute-start.25 = (f32[4,8]{1,0:T(4,128)S(1)}, f32[4,8]{1,0:T(4,128)S(1)}, u32[]{:S(2)}, u32[]{:S(2)}) collective-permute-start(f32[4,8]{1,0:T(4,128)S(1)} %add.46), channel_id=1, source_target_pairs={{0,4},{1,5},{2,6},{3,7},{4,0},{5,1},{6,2},{7,3},{8,12},{9,13},{10,... | collective-permute-start | bytes 392 | tf_op jit(solution)/shard_map/ppermute | solution.py:277
  125.4 4.5 %copy-start.2 = (s32[8]{0:T(128)S(1)}, s32[8]{0:T(128)}, u32[]{:S(2)}) copy-start(s32[8]{0:T(128)} %param.9) | copy-start | bytes 100
  125.4 4.5 %copy-start.3 = (s32[1,4]{1,0:T(1,128)S(1)}, s32[1,4]{1,0:T(1,128)}, u32[]{:S(2)}) copy-start(s32[1,4]{1,0:T(1,128)} %param.10) | copy-start | bytes 52
